TPU v7x, 768 devices: a whole 4x8x12 slice. The times are simulated.
768 devices in a mesh: sec: 2 (over y_lo), seq: 48 (over x, z), mp: 8 (over y_hi, core).
Axes of the slice: x: 4, y: 8 (y_hi: 4, y_lo: 2; y = y_hi * 2 + y_lo), z: 12, core: 2. Of those that a mesh axis runs over, the one named last changes fastest.
Arguments:
- queries: bfloat16 [12288, 2048], P(('sec', 'seq'), 'mp'), may hold values from -6 to 6
- keys_values: bfloat16 [2, 192, 2048], P(None, ('sec', 'seq'), 'mp'), may hold values from -6 to 6
- out_grad: bfloat16 [12288, 4096], P(('sec', 'seq'), 'mp'), may hold values from -6 to 6
- out_weight: bfloat16 [2048, 4096], P('mp'), may hold values from -0.125 to 0.125
- enc_len: int32 [2], replicated, may hold values from 48 to 96
- dec_len: int32 [2], replicated, may hold values from 1 to 6144
Outputs:
- query_grad: bfloat16 [12288, 2048], P(('sec', 'seq'), 'mp')
- key_value_grad: bfloat16 [2, 192, 2048], P(None, ('sec', 'seq'), 'mp')
All inputs are finite; a program needn't handle non-finite values.
Results may differ from a plain program's by a relative error of at most 0.014.
Values may be sent and summed in bfloat16 or wider, within the bound.
No kernel may reach another device: no remote copies, remote signals or barrier semaphores. Data moves between devices by JAX's collectives and lax.ppermute only.
A program may use at most 32 MiB of HBM per device.

v0:
```python
import jax
import jax.numpy as jnp
from jax import lax
from jax.sharding import PartitionSpec as P

DH = 256
SEQS = 2


def body(queries, keys_values, out_grad, out_weight, enc_len, dec_len):
    score_scale = DH ** (-0.5)
    query_rows = queries.shape[0]
    local_width = queries.shape[1]
    heads_here = local_width // DH
    groups = lax.axis_size(("sec", "seq"))
    own_keys = keys_values.shape[1]
    total_k = own_keys * groups
    per_query_seq = query_rows * groups // SEQS
    per_key_seq = total_k // SEQS
    seq_ids = jnp.arange(SEQS, dtype=jnp.int32)
    query_pos = lax.axis_index(("sec", "seq")) * query_rows + jnp.arange(
        query_rows, dtype=jnp.int32
    )
    query_seg = query_pos // per_query_seq
    dec_limit = jnp.sum(
        jnp.where(query_seg[:, None] == seq_ids[None, :], dec_len[None, :], 0), axis=1
    )
    query_valid = query_pos % per_query_seq < dec_limit
    full_grad = lax.all_gather(out_grad, "mp", axis=1, tiled=True)
    grad_flat = jnp.dot(full_grad, out_weight.T, preferred_element_type=jnp.float32).astype(
        jnp.bfloat16
    )
    grad_flat = jnp.where(query_valid[:, None], grad_flat, jnp.zeros_like(grad_flat))
    q_heads = queries.reshape(query_rows, heads_here, DH)
    g_heads = grad_flat.reshape(query_rows, heads_here, DH)
    key_base = lax.axis_index("sec") * own_keys * lax.axis_size("seq")

    def allowed_for(key_width):
        key_pos = key_base + jnp.arange(key_width, dtype=jnp.int32)
        key_seg = key_pos // per_key_seq
        enc_limit = jnp.sum(
            jnp.where(key_seg[:, None] == seq_ids[None, :], enc_len[None, :], 0), axis=1
        )
        key_valid = key_pos % per_key_seq < enc_limit
        return (query_seg[:, None] == key_seg[None, :]) & key_valid[None, :]

    def scores_for(kv_block):
        key_width = kv_block.shape[1]
        k_heads = kv_block[0].reshape(key_width, heads_here, DH)
        v_heads = kv_block[1].reshape(key_width, heads_here, DH)
        scores = (
            jnp.einsum("qhd,khd->hqk", q_heads, k_heads, preferred_element_type=jnp.float32)
            * score_scale
        )
        allowed = allowed_for(key_width)[None]
        return (jnp.where(allowed, scores, -1e30), allowed, k_heads, v_heads)

    run_max = jnp.full((heads_here, query_rows), -1e30, jnp.float32)
    scores, allowed, k_heads, v_heads = scores_for(
        lax.all_gather(keys_values, "seq", axis=1, tiled=True)
    )
    new_max = jnp.maximum(run_max, jnp.max(scores, axis=2))
    expo_terms = jnp.where(allowed, jnp.exp(scores - new_max[..., None]), 0.0)
    run_total = jnp.sum(expo_terms, axis=2)
    weighted = jnp.einsum(
        "hqk,khd->hqd", expo_terms, v_heads.astype(jnp.float32), precision=lax.Precision.HIGHEST
    )
    run_max, run_total, weighted = (new_max, run_total, weighted)
    log_total = run_max + jnp.log(run_total)
    attn_out = weighted / run_total[..., None]
    row_delta = jnp.sum(jnp.transpose(g_heads.astype(jnp.float32), (1, 0, 2)) * attn_out, axis=2)
    kv_block = lax.all_gather(keys_values, "seq", axis=1, tiled=True)
    key_width = kv_block.shape[1]
    scores, allowed, k_heads, v_heads = scores_for(kv_block)
    attn_prob = jnp.where(allowed, jnp.exp(scores - log_total[..., None]), 0.0)
    grad_prob = jnp.einsum("qhd,khd->hqk", g_heads, v_heads, preferred_element_type=jnp.float32)
    grad_score = (attn_prob * (grad_prob - row_delta[..., None])).astype(jnp.bfloat16)
    grad_q = jnp.einsum("hqk,khd->hqd", grad_score, k_heads, preferred_element_type=jnp.float32)
    grad_key = (
        jnp.einsum("hqk,qhd->khd", grad_score, q_heads, preferred_element_type=jnp.float32)
        * score_scale
    )
    grad_value = jnp.einsum(
        "hqk,qhd->khd", attn_prob.astype(jnp.bfloat16), g_heads, preferred_element_type=jnp.float32
    )
    key_panel = jnp.stack(
        [grad_key.reshape(key_width, local_width), grad_value.reshape(key_width, local_width)]
    )
    grad_kv = key_panel
    grad_q, grad_kv = (grad_q, grad_kv)
    query_grad = (
        jnp.transpose(grad_q * score_scale, (1, 0, 2))
        .reshape(query_rows, local_width)
        .astype(jnp.bfloat16)
    )
    owned = lax.psum_scatter(grad_kv, "seq", scatter_dimension=1, tiled=True)
    return (query_grad, owned.astype(jnp.bfloat16))


def solution(mesh):
    placed = (
        P(("sec", "seq"), "mp"),
        P(None, ("sec", "seq"), "mp"),
        P(("sec", "seq"), "mp"),
        P("mp", None),
        P(),
        P(),
    )
    return jax.shard_map(
        body,
        mesh=mesh,
        in_specs=placed,
        out_specs=(P(("sec", "seq"), "mp"), P(None, ("sec", "seq"), "mp")),
        check_vma=False,
    )
```

profile of v0, /device:TPU:56, one launch (start us, length us, event | category | flops | bytes accessed | tf_op | source)
XLA Modules:
  0.0 317.0 jit_solution(18324062005554043675)
XLA Ops:
  7.2 0.0 copy-start
  7.2 0.0 all-gather.2.cloned.1.call-start
  7.2 0.7 all-gather.2.cloned.1.call-update
  7.9 0.7 copy.12
  8.6 1.3 dynamic-slice
  10.6 83.8 %all_gather.7 = bf16[2,96,256]{2,0,1:T(2,128)(2,1)S(1)} all-gather(bf16[2,2,256]{2,0,1:T(2,128)(2,1)S(1)} %copy.12), channel_id=1, replica_groups=mesh['sec'=2,'seq'=48,'mp'=8] {'seq'}, dimensions={1}, use_global_device_ids=true | all-gather | bytes 100352 | tf_op jit(solution)/shard_map/all_gather | solution.py:72
  94.3 0.7 fusion.22
  95.1 0.7 fusion.21
  95.8 0.1 fusion.29
  96.0 1.0 fusion.30
  97.0 0.1 fusion.8
  97.1 0.0 copy-start.1
  97.2 0.0 all-gather.2.cloned.1.call-done
  97.2 0.0 copy-done
  97.2 2.1 fusion.4
  99.3 0.4 fusion.3
  99.7 0.2 convolution_bitcast_fusion
  99.9 0.2 fusion.7
  100.1 0.8 fusion.2
  100.9 0.0 copy-done.1
  100.9 0.1 fusion.1
  101.1 208.5 %all-reduce.2 = bf16[2,96,256]{2,1,0:T(8,128)(2,1)S(1)} all-reduce(f32[2,96,256]{2,1,0:T(8,128)S(1)} %pad_maximum_fusion), channel_id=2, replica_groups=mesh['sec'=2,'seq'=48,'mp'=8] {'seq'}, use_global_device_ids=true, to_apply=%region_5.6.clone | all-reduce | flops 49152 | bytes 294912
  309.6 0.6 dynamic-slice_convert_fusion
  (7 shorter events, 0.1 us)
Async XLA Ops:
  7.2 90.0 %copy-start = (bf16[256,4096]{1,0:T(8,128)(2,1)S(1)}, bf16[256,4096]{1,0:T(8,128)(2,1)}, u32[]{:S(2)}) copy-start(bf16[256,4096]{1,0:T(8,128)(2,1)} %param.9) | copy-start | bytes 6291460
  7.2 90.0 %all-gather.2.cloned.1.call-start = ((), (), s32[]{:S(2)}) async-start(), calls=%async_computation | async-start | bytes 1179648 | tf_op jit(solution)/shard_map/all_gather | solution.py:29
  97.1 3.8 %copy-start.1 = (bf16[128,256]{1,0:T(8,128)(2,1)S(1)}, bf16[128,256]{1,0:T(8,128)(2,1)}, u32[]{:S(2)}) copy-start(bf16[128,256]{1,0:T(8,128)(2,1)} %param.6) | copy-start | bytes 196612
Sparse Core Ops, SparseCore 0:
  10.4 39.0 all-gather.1
where the time goes:
time: 317 us
  blocking collectives  292 us (92%)
  between operations  14.8 us (5%)
  matrix products  4.85 us (2%)
    unnamed x1, blocking collectives  209 us
    all_gather x1, blocking collectives, body(): kv_block = lax.all_gather(keys_values, 'seq', axis=1, tiled=True)  83.8 us
  transfers between devices with their start and end apart: 1, of which 0 were waited for; matrix products, arithmetic and copies ran while one was open for 2% of the time, Pallas kernels for 0%

commit v1 on v0

v1 whole, which is shorter than its diff:
```python
import jax
import jax.numpy as jnp
from jax import lax
from jax.experimental import pallas as pl
from jax.experimental.pallas import tpu as pltpu
from jax.sharding import Mesh, PartitionSpec as P

DH = 256
SEQS = 2
F32 = jnp.float32
BF16 = jnp.bfloat16
VMEM = pl.BlockSpec(memory_space=pltpu.VMEM)
SMEM = pl.BlockSpec(memory_space=pltpu.SMEM)
PARAMS = pltpu.CompilerParams(vmem_limit_bytes=32 * 1024 * 1024)


def dot_nt(a, b):
    return lax.dot_general(a, b, (((1,), (1,)), ((), ())), preferred_element_type=F32)


def dot_tn(a, b):
    return lax.dot_general(a, b, (((0,), (0,)), ((), ())), preferred_element_type=F32)


def masked_softmax(scores, allowed):
    scores = jnp.where(allowed, scores, -1e30)
    expo = jnp.where(allowed, jnp.exp(scores - jnp.max(scores, axis=1, keepdims=True)), 0.0)
    return expo / jnp.sum(expo, axis=1, keepdims=True)


def project(og_ref, w_ref, core):
    chips, rows, slab = og_ref.shape
    total = jnp.zeros((rows, DH), F32)
    for chip in range(chips):
        first = pl.multiple_of((2 * chip + core) * slab, slab)
        total += dot_nt(og_ref[chip], w_ref[:, pl.ds(first, slab)])
    return total


def before_kernel(nums_ref, og_ref, w_ref, q_ref, kv_ref, part_ref, pk_ref, pv_ref, sw_ref, *, own):
    rows = og_ref.shape[1]
    total = kv_ref.shape[0]
    enc_limit = nums_ref[0]
    part_ref[...] = project(og_ref, w_ref, nums_ref[2])
    q = q_ref[...]
    kv = kv_ref[...]
    r = lax.broadcasted_iota(jnp.int32, (total, total), 0)
    c = lax.broadcasted_iota(jnp.int32, (total, total), 1)
    partner = jnp.where((r % (2 * own)) < own, r + own, r - own)
    swap = jnp.where(c == partner, 1.0, 0.0).astype(BF16)
    swapped = jnp.dot(swap, kv, preferred_element_type=F32).astype(BF16)
    sw_ref[...] = swapped
    scale = DH ** (-0.5)
    col = lax.broadcasted_iota(jnp.int32, (rows, total), 1)
    is_key = (col % (2 * own)) < own
    inside = (col // (2 * own)) * own + col % own < enc_limit
    pk_ref[...] = masked_softmax(dot_nt(q, kv) * scale, is_key & inside)
    pv_ref[...] = masked_softmax(
        dot_nt(q, swapped) * scale, jnp.logical_not(is_key) & inside
    ).astype(BF16)


def after_kernel(
    nums_ref, og_ref, w_ref, q_ref, kv_ref, part_ref, pk_ref, pv_ref, sw_ref, dq_ref, panel_ref
):
    rows = og_ref.shape[1]
    scale = DH ** (-0.5)
    grad = part_ref[...] + project(og_ref, w_ref, 1 - nums_ref[2])
    row = lax.broadcasted_iota(jnp.int32, (rows, DH), 0)
    g = jnp.where(row < nums_ref[1], grad, 0.0).astype(BF16)
    prob = pk_ref[...]
    grad_prob = dot_nt(g, sw_ref[...])
    delta = jnp.sum(prob * grad_prob, axis=1, keepdims=True)
    grad_score = (prob * (grad_prob - delta)).astype(BF16)
    panel = dot_tn(grad_score, q_ref[...]) * scale + dot_tn(pv_ref[...], g)
    panel_ref[...] = panel.astype(BF16)
    dq_ref[...] = (jnp.dot(grad_score, kv_ref[...], preferred_element_type=F32) * scale).astype(BF16)


def sum_kernel(parts_ref, out_ref):
    out_ref[...] = jnp.sum(parts_ref[...].astype(F32), axis=0).astype(BF16)


def body(queries, keys_values, out_grad, out_weight, enc_len, dec_len):
    rows = queries.shape[0]
    own = keys_values.shape[1]
    seq = ("sx", "sz")
    groups = lax.axis_size(seq)
    total = 2 * own * groups
    sec = lax.axis_index("sec")
    nums = jnp.stack(
        [enc_len[sec], dec_len[sec] - lax.axis_index(seq) * rows, lax.axis_index("mc")]
    )
    kv_mine = keys_values.reshape(1, 2 * own, DH)
    kv = lax.all_to_all(
        jnp.broadcast_to(kv_mine, (groups, 2 * own, DH)), seq, 0, 0, tiled=True
    ).reshape(total, DH)
    og, kv = lax.optimization_barrier((lax.all_gather(out_grad, "my", axis=0), kv))
    og_other = lax.ppermute(og, "mc", [(0, 1), (1, 0)])
    before = pl.pallas_call(
        lambda *refs: before_kernel(*refs, own=own),
        name="softmax_and_own_columns",
        out_shape=(
            jax.ShapeDtypeStruct((rows, DH), F32),
            jax.ShapeDtypeStruct((rows, total), F32),
            jax.ShapeDtypeStruct((rows, total), BF16),
            jax.ShapeDtypeStruct((total, DH), BF16),
        ),
        in_specs=[SMEM, VMEM, VMEM, VMEM, VMEM],
        out_specs=(VMEM,) * 4,
        compiler_params=PARAMS,
    )(nums, og, out_weight, queries, kv)
    query_grad, panel = pl.pallas_call(
        after_kernel,
        name="gradients",
        out_shape=(
            jax.ShapeDtypeStruct((rows, DH), BF16),
            jax.ShapeDtypeStruct((total, DH), BF16),
        ),
        in_specs=[SMEM] + [VMEM] * 8,
        out_specs=(VMEM, VMEM),
        compiler_params=PARAMS,
    )(nums, og_other, out_weight, queries, kv, *before)
    parts = lax.all_to_all(panel.reshape(groups, 2 * own, DH), seq, 0, 0, tiled=True)
    owned = pl.pallas_call(
        sum_kernel,
        name="sum_of_parts",
        out_shape=jax.ShapeDtypeStruct((2 * own, DH), BF16),
        in_specs=[VMEM],
        out_specs=VMEM,
        compiler_params=PARAMS,
    )(parts)
    return query_grad, owned.reshape(2, own, DH)


def solution(mesh):
    sizes = dict(mesh.shape)
    fine = Mesh(
        mesh.devices.reshape(sizes["sec"], 4, sizes["seq"] // 4, sizes["mp"] // 2, 2),
        ("sec", "sx", "sz", "my", "mc"),
    )
    tok, mp = ("sec", "sx", "sz"), ("my", "mc")
    return jax.shard_map(
        body,
        mesh=fine,
        in_specs=(P(tok, mp), P(None, tok, mp), P(tok, mp), P(mp, None), P(), P()),
        out_specs=(P(tok, mp), P(None, tok, mp)),
        check_vma=False,
    )
```

time: 317 us -> 79.1 us (0.25)
  the two profiles are of different devices: /device:TPU:56 before, /device:TPU:1 now
where the time goes in v1:
time: 79.1 us; the launch traced here: 78.7 us
  blocking collectives  40.5 us (51%)
  starting transfers between devices  25.3 us (32%)
  local copies, waits for them, and re-layouts  7.25 us (9%)
  Pallas kernels  3.6 us (5%)
  between operations  1.35 us (2%)
    all_to_all x1, blocking collectives, body(): lax.all_to_all(panel.reshape(groups, 2 * own, DH), seq, 0, 0, tiled=True)  24.5 us
    all_to_all x1, starting transfers between devices, body(): lax.all_to_all(jnp.broadcast_to(kv_mine, (groups, 2 * own, DH)), seq, 0,...  18.8 us
    all_gather x1, blocking collectives, body(): lax.all_gather(out_grad, 'my', axis=0)  15.9 us
    ppermute x1, starting transfers between devices, body(): og_other = lax.ppermute(og, 'mc', [(0, 1), (1, 0)])  6.43 us
    unnamed x8, local copies, waits for them, and re-layouts  2.67 us
    pallas_call x1, Pallas kernels, body(): pl.pallas_call(after_kernel, name='gradients', out_shape=(jax.ShapeDtypeS...  2.2 us
  transfers between devices with their start and end apart: 2, of which 0 were waited for; matrix products, arithmetic and copies ran while one was open for 4% of the time, Pallas kernels for 2%

profile of v1, /device:TPU:1, one launch (start us, length us, event | category | flops | bytes accessed | tf_op | source)
XLA Modules:
  0.0 78.7 jit_solution(18286044498682705083)
XLA Ops:
  0.6 0.0 copy-start.3
  0.6 0.7 broadcast_in_dim.7
  1.4 0.7 broadcast_in_dim.8
  2.0 18.8 %all-to-all-start = ((bf16[48,4,256]{2,1,0:T(4,128)(2,1)}), bf16[48,4,256]{2,1,0:T(4,128)(2,1)S(1)}, u32[]{:S(2)}, u32[]{:S(2)}) async-start(bf16[48,4,256]{2,1,0:T(4,128)(2,1)} %broadcast_in_dim.8), calls=%async_computation | async-start | bytes 196608 | tf_op jit(solution)/shard_map/all_to_all | solution.py:95
  20.9 15.9 %all-gather = bf16[512,512]{1,0:T(8,128)(2,1)S(1)} all-gather(bf16[128,512]{1,0:T(8,128)(2,1)} %param.8), channel_id=2, replica_groups=mesh['sec'=2,'sx'=4,'sz'=12,'my'=4,'mc'=2] {'my'}, dimensions={0}, use_global_device_ids=true | all-gather | bytes 655360 | tf_op jit(solution)/shard_map/all_gather | solution.py:98
  36.8 0.0 all-to-all-done
  36.8 6.4 %collective-permute-start = (bf16[4,128,512]{2,1,0:T(8,128)(2,1)S(1)}, bf16[4,128,512]{2,1,0:T(8,128)(2,1)S(1)}, u32[]{:S(2)}, u32[]{:S(2)}) collective-permute-start(bf16[4,128,512]{2,1,0:T(8,128)(2,1)S(1)} %bitcast.4), channel_id=1, source_target_pairs={{0,1},{1,0},{2,3},{3,2},{4,5},{5,4},{6,7},{7,6},{8,9},{9,8},{10,11... | collective-permute-start | bytes 1572872 | tf_op jit(solution)/shard_map/ppermute | solution.py:99
  43.3 1.2 %dynamic_slice.7 = s32[1]{0:T(128)} dynamic-slice(s32[2]{0:T(128)} %param.11, s32[]{:T(128)S(6)} %select_n.4), dynamic_slice_sizes={1} | dynamic-slice | bytes 12 | tf_op jit(solution)/shard_map/dynamic_slice | solution.py:92
  44.5 1.3 %dynamic_slice.6 = s32[1]{0:T(128)} dynamic-slice(s32[2]{0:T(128)} %param.10, s32[]{:T(128)S(6)} %select_n.4), dynamic_slice_sizes={1} | dynamic-slice | bytes 12 | tf_op jit(solution)/shard_map/dynamic_slice | solution.py:92
  46.5 0.8 pad_add_fusion.refs_0_.nums_ref
  47.3 0.0 copy-start
  47.3 1.6 %copy-done = bf16[256,4096]{1,0:T(8,128)(2,1)S(1)} copy-done((bf16[256,4096]{1,0:T(8,128)(2,1)S(1)}, bf16[256,4096]{1,0:T(8,128)(2,1)}, u32[]{:S(2)}) %copy-start) | copy-done | bytes 2097176
  48.9 0.0 copy-start.2
  48.9 0.8 %copy-done.2 = bf16[128,256]{1,0:T(8,128)(2,1)S(1)} copy-done((bf16[128,256]{1,0:T(8,128)(2,1)S(1)}, bf16[128,256]{1,0:T(8,128)(2,1)}, u32[]{:S(2)}) %copy-start.2) | copy-done | bytes 65560
  49.7 0.0 copy-start.1
  49.7 1.3 %softmax_and_own_columns.1 = (f32[128,256]{1,0:T(8,128)S(1)}, f32[128,192]{1,0:T(8,128)S(1)}, bf16[128,192]{1,0:T(8,128)(2,1)S(1)}, bf16[192,256]{1,0:T(8,128)(2,1)S(1)}) custom-call(s32[3]{0:T(128)S(1)} %pad_add_fusion.refs_0_.nums_ref, bf16[4,128,512]{2,1,0:T(8,128)(2,1)S(1)} %bitcast.5, bf16[256,4096]{1,0:T(8,128)(2,1)S(1)} %copy-done, ...), custom_call_target="tpu_custom_call" | custom-call | tf_op jit(solution)/shard_map/softmax_and_own_columns/pallas_call | solution.py:100
  51.0 0.0 collective-permute-done.og_ref
  51.0 0.0 copy-done.3
  51.1 0.2 copy-done.1
  51.3 2.2 %gradients.1 = (bf16[128,256]{1,0:T(8,128)(2,1)}, bf16[192,256]{1,0:T(8,128)(2,1)S(1)}) custom-call(s32[3]{0:T(128)S(1)} %pad_add_fusion.refs_0_.nums_ref, bf16[4,128,512]{2,1,0:T(8,128)(2,1)S(1)} %collective-permute-done.og_ref, bf16[256,4096]{1,0:T(8,128)(2,1)S(1)} %copy-done.1, bf16[128,256]{1,0:T(8,128)(2,1)S(1)} %copy-done.3, ...), custom_call_target="tpu_custom_call" | custom-call | tf_op jit(solution)/shard_map/gradients/pallas_call | solution.py:113
  53.5 24.5 %all_to_all.10.parts_ref = bf16[48,4,256]{2,1,0:T(4,128)(2,1)S(1)} all-to-all(bf16[48,4,256]{2,1,0:T(4,128)(2,1)S(1)} %reshape.16), channel_id=1, replica_groups=mesh['sec'=2,'sx'=4,'sz'=12,'my'=4,'mc'=2] {'sx','sz'}, dimensions={0} | all-to-all | bytes 196608 | tf_op jit(solution)/shard_map/all_to_all | solution.py:124
  78.0 0.1 sum_of_parts.1
  78.1 0.6 reshape.17
  (2 shorter events, 0.1 us)
Async XLA Ops:
  0.6 50.4 %copy-start.3 = (bf16[128,256]{1,0:T(8,128)(2,1)S(1)}, bf16[128,256]{1,0:T(8,128)(2,1)}, u32[]{:S(2)}) copy-start(bf16[128,256]{1,0:T(8,128)(2,1)} %q_ref.1) | copy-start | bytes 196612
  2.0 34.8 %all-to-all-start = ((bf16[48,4,256]{2,1,0:T(4,128)(2,1)}), bf16[48,4,256]{2,1,0:T(4,128)(2,1)S(1)}, u32[]{:S(2)}, u32[]{:S(2)}) async-start(bf16[48,4,256]{2,1,0:T(4,128)(2,1)} %broadcast_in_dim.8), calls=%async_computation | async-start | bytes 196608 | tf_op jit(solution)/shard_map/all_to_all | solution.py:95
  36.8 14.2 %collective-permute-start = (bf16[4,128,512]{2,1,0:T(8,128)(2,1)S(1)}, bf16[4,128,512]{2,1,0:T(8,128)(2,1)S(1)}, u32[]{:S(2)}, u32[]{:S(2)}) collective-permute-start(bf16[4,128,512]{2,1,0:T(8,128)(2,1)S(1)} %bitcast.4), channel_id=1, source_target_pairs={{0,1},{1,0},{2,3},{3,2},{4,5},{5,4},{6,7},{7,6},{8,9},{9,8},{10,11... | collective-permute-start | bytes 1572872 | tf_op jit(solution)/shard_map/ppermute | solution.py:99
  47.3 1.6 %copy-start = (bf16[256,4096]{1,0:T(8,128)(2,1)S(1)}, bf16[256,4096]{1,0:T(8,128)(2,1)}, u32[]{:S(2)}) copy-start(bf16[256,4096]{1,0:T(8,128)(2,1)} %w_ref.1) | copy-start | bytes 6291460
  48.9 0.8 %copy-start.2 = (bf16[128,256]{1,0:T(8,128)(2,1)S(1)}, bf16[128,256]{1,0:T(8,128)(2,1)}, u32[]{:S(2)}) copy-start(bf16[128,256]{1,0:T(8,128)(2,1)} %q_ref.1) | copy-start | bytes 196612
  49.7 1.6 %copy-start.1 = (bf16[256,4096]{1,0:T(8,128)(2,1)S(1)}, bf16[256,4096]{1,0:T(8,128)(2,1)}, u32[]{:S(2)}) copy-start(bf16[256,4096]{1,0:T(8,128)(2,1)} %w_ref.1) | copy-start | bytes 6291460

commit v2 on v1

--- a/solution.py
+++ b/solution.py
@@ -10,7 +10,7 @@
 F32 = jnp.float32
 BF16 = jnp.bfloat16
 VMEM = pl.BlockSpec(memory_space=pltpu.VMEM)
-SMEM = pl.BlockSpec(memory_space=pltpu.SMEM)
+HBM = pl.BlockSpec(memory_space=pltpu.HBM)
 PARAMS = pltpu.CompilerParams(vmem_limit_bytes=32 * 1024 * 1024)
 
 
@@ -37,12 +37,21 @@
     return total
 
 
-def before_kernel(nums_ref, og_ref, w_ref, q_ref, kv_ref, part_ref, pk_ref, pv_ref, sw_ref, *, own):
-    rows = og_ref.shape[1]
-    total = kv_ref.shape[0]
-    enc_limit = nums_ref[0]
-    part_ref[...] = project(og_ref, w_ref, nums_ref[2])
-    q = q_ref[...]
+def before_kernel(
+    enc_hbm, dec_hbm, w_hbm, q_hbm, og_ref, kv_ref,
+    w_ref, q_ref, part_ref, mask_ref, pk_ref, pv_ref, sw_ref,
+    enc_ref, dec_ref, sems, *, own,
+):
+    copies = [
+        pltpu.make_async_copy(src, dst, sems.at[i])
+        for i, (src, dst) in enumerate(
+            ((enc_hbm, enc_ref), (dec_hbm, dec_ref), (q_hbm, q_ref), (w_hbm, w_ref))
+        )
+    ]
+    for copy in copies:
+        copy.start()
+    rows, total = pk_ref.shape
+    sec = lax.axis_index("sec")
     kv = kv_ref[...]
     r = lax.broadcasted_iota(jnp.int32, (total, total), 0)
     c = lax.broadcasted_iota(jnp.int32, (total, total), 1)
@@ -51,6 +60,10 @@
     swapped = jnp.dot(swap, kv, preferred_element_type=F32).astype(BF16)
     sw_ref[...] = swapped
     scale = DH ** (-0.5)
+    for copy in copies[:3]:
+        copy.wait()
+    q = q_ref[...]
+    enc_limit = enc_ref[sec]
     col = lax.broadcasted_iota(jnp.int32, (rows, total), 1)
     is_key = (col % (2 * own)) < own
     inside = (col // (2 * own)) * own + col % own < enc_limit
@@ -58,16 +71,19 @@
     pv_ref[...] = masked_softmax(
         dot_nt(q, swapped) * scale, jnp.logical_not(is_key) & inside
     ).astype(BF16)
+    valid_rows = dec_ref[sec] - lax.axis_index(("sx", "sz")) * rows
+    row = lax.broadcasted_iota(jnp.int32, (rows, DH), 0)
+    mask_ref[...] = jnp.where(row < valid_rows, 1.0, 0.0)
+    copies[3].wait()
+    part_ref[...] = project(og_ref, w_ref, lax.axis_index("mc"))
 
 
 def after_kernel(
-    nums_ref, og_ref, w_ref, q_ref, kv_ref, part_ref, pk_ref, pv_ref, sw_ref, dq_ref, panel_ref
+    og_ref, kv_ref, w_ref, q_ref, part_ref, mask_ref, pk_ref, pv_ref, sw_ref, dq_ref, panel_ref
 ):
-    rows = og_ref.shape[1]
     scale = DH ** (-0.5)
-    grad = part_ref[...] + project(og_ref, w_ref, 1 - nums_ref[2])
-    row = lax.broadcasted_iota(jnp.int32, (rows, DH), 0)
-    g = jnp.where(row < nums_ref[1], grad, 0.0).astype(BF16)
+    grad = part_ref[...] + project(og_ref, w_ref, 1 - lax.axis_index("mc"))
+    g = jnp.where(mask_ref[...] > 0.0, grad, 0.0).astype(BF16)
     prob = pk_ref[...]
     grad_prob = dot_nt(g, sw_ref[...])
     delta = jnp.sum(prob * grad_prob, axis=1, keepdims=True)
@@ -78,7 +94,10 @@
 
 
 def sum_kernel(parts_ref, out_ref):
-    out_ref[...] = jnp.sum(parts_ref[...].astype(F32), axis=0).astype(BF16)
+    total = jnp.sum(parts_ref[...].astype(F32), axis=0).astype(BF16)
+    own = out_ref.shape[1]
+    out_ref[0] = total[:own]
+    out_ref[1] = total[own:]
 
 
 def body(queries, keys_values, out_grad, out_weight, enc_len, dec_len):
@@ -87,29 +106,32 @@
     seq = ("sx", "sz")
     groups = lax.axis_size(seq)
     total = 2 * own * groups
-    sec = lax.axis_index("sec")
-    nums = jnp.stack(
-        [enc_len[sec], dec_len[sec] - lax.axis_index(seq) * rows, lax.axis_index("mc")]
-    )
-    kv_mine = keys_values.reshape(1, 2 * own, DH)
     kv = lax.all_to_all(
-        jnp.broadcast_to(kv_mine, (groups, 2 * own, DH)), seq, 0, 0, tiled=True
+        jnp.broadcast_to(keys_values[None], (groups, 2, own, DH)), seq, 0, 0, tiled=True
     ).reshape(total, DH)
     og, kv = lax.optimization_barrier((lax.all_gather(out_grad, "my", axis=0), kv))
     og_other = lax.ppermute(og, "mc", [(0, 1), (1, 0)])
-    before = pl.pallas_call(
+    kept = pl.pallas_call(
         lambda *refs: before_kernel(*refs, own=own),
         name="softmax_and_own_columns",
         out_shape=(
+            jax.ShapeDtypeStruct(out_weight.shape, BF16),
+            jax.ShapeDtypeStruct((rows, DH), BF16),
+            jax.ShapeDtypeStruct((rows, DH), F32),
             jax.ShapeDtypeStruct((rows, DH), F32),
             jax.ShapeDtypeStruct((rows, total), F32),
             jax.ShapeDtypeStruct((rows, total), BF16),
             jax.ShapeDtypeStruct((total, DH), BF16),
         ),
-        in_specs=[SMEM, VMEM, VMEM, VMEM, VMEM],
-        out_specs=(VMEM,) * 4,
+        in_specs=[HBM] * 4 + [VMEM] * 2,
+        out_specs=(VMEM,) * 7,
+        scratch_shapes=[
+            pltpu.SMEM(enc_len.shape, jnp.int32),
+            pltpu.SMEM(dec_len.shape, jnp.int32),
+            pltpu.SemaphoreType.DMA((4,)),
+        ],
         compiler_params=PARAMS,
-    )(nums, og, out_weight, queries, kv)
+    )(enc_len, dec_len, out_weight, queries, og, kv)
     query_grad, panel = pl.pallas_call(
         after_kernel,
         name="gradients",
@@ -117,20 +139,20 @@
             jax.ShapeDtypeStruct((rows, DH), BF16),
             jax.ShapeDtypeStruct((total, DH), BF16),
         ),
-        in_specs=[SMEM] + [VMEM] * 8,
+        in_specs=[VMEM] * 9,
         out_specs=(VMEM, VMEM),
         compiler_params=PARAMS,
-    )(nums, og_other, out_weight, queries, kv, *before)
+    )(og_other, kv, *kept)
     parts = lax.all_to_all(panel.reshape(groups, 2 * own, DH), seq, 0, 0, tiled=True)
     owned = pl.pallas_call(
         sum_kernel,
         name="sum_of_parts",
-        out_shape=jax.ShapeDtypeStruct((2 * own, DH), BF16),
+        out_shape=jax.ShapeDtypeStruct((2, own, DH), BF16),
         in_specs=[VMEM],
         out_specs=VMEM,
         compiler_params=PARAMS,
     )(parts)
-    return query_grad, owned.reshape(2, own, DH)
+    return query_grad, owned
 
 
 def solution(mesh):

time: 79.1 us -> 75.8 us (0.958)
  local copies, waits for them, and re-layouts: 7.25 us -> 5.17 us
    dynamic_slice x2 -> x0, local copies, waits for them, and re-layouts: 2.55 us -> none  [the longest x1 1.31 us: body(): enc_len[sec]]
    unnamed x8, local copies, waits for them, and re-layouts: 2.67 us -> 3.73 us
  transfers between devices with their start and end apart: 2 -> 2, of which waited for: 0 -> 0; matrix products, arithmetic and copies ran while one was open for 4% -> 0% of each run, Pallas kernels for 2% -> 2%
where the time goes in v2:
time: 75.8 us; the launch traced here: 75.4 us
  blocking collectives  40.5 us (53%)
  starting transfers between devices  25.3 us (33%)
  local copies, waits for them, and re-layouts  5.17 us (7%)
  Pallas kernels  3.85 us (5%)
    all_to_all x1, blocking collectives, body(): lax.all_to_all(panel.reshape(groups, 2 * own, DH), seq, 0, 0, tiled=True)  24.5 us
    all_to_all x1, starting transfers between devices, body(): lax.all_to_all(jnp.broadcast_to(keys_values[None], (groups, 2, own, DH)),...  18.8 us
    all_gather x1, blocking collectives, body(): lax.all_gather(out_grad, 'my', axis=0)  15.9 us
    ppermute x1, starting transfers between devices, body(): og_other = lax.ppermute(og, 'mc', [(0, 1), (1, 0)])  6.43 us
    unnamed x8, local copies, waits for them, and re-layouts  3.73 us
    pallas_call x1, Pallas kernels, body(): pl.pallas_call(after_kernel, name='gradients', out_shape=(jax.ShapeDtypeS...  1.66 us
    pallas_call x1, Pallas kernels, body(): pl.pallas_call(lambda *refs: before_kernel(*refs, own=own), name='softmax...  1.55 us
  transfers between devices with their start and end apart: 2, of which 0 were waited for; matrix products, arithmetic and copies ran while one was open for 0% of the time, Pallas kernels for 2%

profile of v2, /device:TPU:1, one launch (start us, length us, event | category | flops | bytes accessed | tf_op | source)
XLA Modules:
  0.0 75.4 jit_solution(10122182113139675328)
XLA Ops:
  0.6 1.4 %broadcast_in_dim.2 = bf16[48,2,2,256]{3,2,1,0:T(2,128)(2,1)} broadcast(bf16[2,2,256]{2,1,0:T(2,128)(2,1)} %param.7), dimensions={1,2,3} | broadcast | bytes 100352 | tf_op jit(solution)/shard_map/broadcast_in_dim | solution.py:110
  2.0 18.8 %all-to-all-start = ((bf16[48,2,2,256]{3,2,1,0:T(2,128)(2,1)}), bf16[48,2,2,256]{3,2,1,0:T(2,128)(2,1)S(1)}, u32[]{:S(2)}, u32[]{:S(2)}) async-start(bf16[48,2,2,256]{3,2,1,0:T(2,128)(2,1)} %broadcast_in_dim.2), calls=%async_computation | async-start | bytes 196608 | tf_op jit(solution)/shard_map/all_to_all | solution.py:109
  20.8 15.9 %all-gather = bf16[512,512]{1,0:T(8,128)(2,1)S(1)} all-gather(bf16[128,512]{1,0:T(8,128)(2,1)} %param.8), channel_id=2, replica_groups=mesh['sec'=2,'sx'=4,'sz'=12,'my'=4,'mc'=2] {'my'}, dimensions={0}, use_global_device_ids=true | all-gather | bytes 655360 | tf_op jit(solution)/shard_map/all_gather | solution.py:112
  36.8 0.0 all-to-all-done
  36.8 6.4 %collective-permute-start = (bf16[4,128,512]{2,1,0:T(8,128)(2,1)S(1)}, bf16[4,128,512]{2,1,0:T(8,128)(2,1)S(1)}, u32[]{:S(2)}, u32[]{:S(2)}) collective-permute-start(bf16[4,128,512]{2,1,0:T(8,128)(2,1)S(1)} %bitcast.1), channel_id=1, source_target_pairs={{0,1},{1,0},{2,3},{3,2},{4,5},{5,4},{6,7},{7,6},{8,9},{9,8},{10,11... | collective-permute-start | bytes 1572872 | tf_op jit(solution)/shard_map/ppermute | solution.py:113
  43.3 0.0 copy-start
  43.3 1.6 %copy-done = bf16[256,4096]{1,0:T(8,128)(2,1)S(1)} copy-done((bf16[256,4096]{1,0:T(8,128)(2,1)S(1)}, bf16[256,4096]{1,0:T(8,128)(2,1)}, u32[]{:S(2)}) %copy-start) | copy-done | bytes 2097176
  44.9 0.0 copy-start.1
  44.9 0.8 %copy-done.1 = bf16[128,256]{1,0:T(8,128)(2,1)S(1)} copy-done((bf16[128,256]{1,0:T(8,128)(2,1)S(1)}, bf16[128,256]{1,0:T(8,128)(2,1)}, u32[]{:S(2)}) %copy-start.1) | copy-done | bytes 65560
  45.7 0.0 copy-start.2
  45.7 0.7 copy-done.2
  46.4 0.0 copy-start.3
  46.4 0.7 copy-done.3
  47.0 1.5 %softmax_and_own_columns.1 = (bf16[256,4096]{1,0:T(8,128)(2,1)S(1)}, bf16[128,256]{1,0:T(8,128)(2,1)S(1)}, f32[128,256]{1,0:T(8,128)S(1)}, f32[128,256]{1,0:T(8,...) custom-call(s32[2]{0:T(128)S(1)} %copy-done.2, s32[2]{0:T(128)S(1)} %copy-done.3, ...), custom_call_target="tpu_custom_call" | custom-call | tf_op jit(solution)/shard_map/softmax_and_own_columns/pallas_call | solution.py:114
  48.6 0.0 collective-permute-done.og_ref
  48.6 1.7 %gradients.1 = (bf16[128,256]{1,0:T(8,128)(2,1)}, bf16[192,256]{1,0:T(8,128)(2,1)S(1)}) custom-call(bf16[4,128,512]{2,1,0:T(8,128)(2,1)S(1)} %collective-permute-done.og_ref, bf16[192,256]{1,0:T(8,128)(2,1)S(1)} %reshape.11.refs_5_.kv_ref, bf16[256,4096]{1,0:T(8,128)(2,1)S(1)} %get-tuple-element.15.w_ref, bf16[128,256]{1,0:T(8,128)(2,1)S(1)} %get-tuple-element.16.q_ref, ...), custom_call_target="tpu_custom_call" | custom-call | tf_op jit(solution)/shard_map/gradients/pallas_call | solution.py:135
  50.3 24.5 %all_to_all.10.parts_ref = bf16[48,4,256]{2,1,0:T(4,128)(2,1)S(1)} all-to-all(bf16[48,4,256]{2,1,0:T(4,128)(2,1)S(1)} %reshape.12), channel_id=1, replica_groups=mesh['sec'=2,'sx'=4,'sz'=12,'my'=4,'mc'=2] {'sx','sz'}, dimensions={0} | all-to-all | bytes 196608 | tf_op jit(solution)/shard_map/all_to_all | solution.py:146
  74.8 0.6 sum_of_parts.1
  (2 shorter events, 0.1 us)
Async XLA Ops:
  2.0 34.8 %all-to-all-start = ((bf16[48,2,2,256]{3,2,1,0:T(2,128)(2,1)}), bf16[48,2,2,256]{3,2,1,0:T(2,128)(2,1)S(1)}, u32[]{:S(2)}, u32[]{:S(2)}) async-start(bf16[48,2,2,256]{3,2,1,0:T(2,128)(2,1)} %broadcast_in_dim.2), calls=%async_computation | async-start | bytes 196608 | tf_op jit(solution)/shard_map/all_to_all | solution.py:109
  36.8 11.7 %collective-permute-start = (bf16[4,128,512]{2,1,0:T(8,128)(2,1)S(1)}, bf16[4,128,512]{2,1,0:T(8,128)(2,1)S(1)}, u32[]{:S(2)}, u32[]{:S(2)}) collective-permute-start(bf16[4,128,512]{2,1,0:T(8,128)(2,1)S(1)} %bitcast.1), channel_id=1, source_target_pairs={{0,1},{1,0},{2,3},{3,2},{4,5},{5,4},{6,7},{7,6},{8,9},{9,8},{10,11... | collective-permute-start | bytes 1572872 | tf_op jit(solution)/shard_map/ppermute | solution.py:113
  43.3 1.6 %copy-start = (bf16[256,4096]{1,0:T(8,128)(2,1)S(1)}, bf16[256,4096]{1,0:T(8,128)(2,1)}, u32[]{:S(2)}) copy-start(bf16[256,4096]{1,0:T(8,128)(2,1)} %refs_2_.1) | copy-start | bytes 6291460
  44.9 0.8 %copy-start.1 = (bf16[128,256]{1,0:T(8,128)(2,1)S(1)}, bf16[128,256]{1,0:T(8,128)(2,1)}, u32[]{:S(2)}) copy-start(bf16[128,256]{1,0:T(8,128)(2,1)} %refs_3_.1) | copy-start | bytes 196612
  45.7 0.7 copy-start.2
  46.4 0.7 copy-start.3

commit v3 on v2

--- a/solution.py
+++ b/solution.py
@@ -100,6 +100,10 @@
     out_ref[1] = total[own:]
 
 
+def in_hbm(x):
+    return pltpu.with_memory_space_constraint(x, pltpu.HBM)
+
+
 def body(queries, keys_values, out_grad, out_weight, enc_len, dec_len):
     rows = queries.shape[0]
     own = keys_values.shape[1]
@@ -131,7 +135,7 @@
             pltpu.SemaphoreType.DMA((4,)),
         ],
         compiler_params=PARAMS,
-    )(enc_len, dec_len, out_weight, queries, og, kv)
+    )(*map(in_hbm, (enc_len, dec_len, out_weight, queries)), og, kv)
     query_grad, panel = pl.pallas_call(
         after_kernel,
         name="gradients",

time: 75.8 us -> 72.7 us (0.959)
  local copies, waits for them, and re-layouts: 5.17 us -> 1.44 us
    unnamed x8 -> x0, local copies, waits for them, and re-layouts: 3.73 us -> none
  transfers between devices with their start and end apart: 2 -> 2, of which waited for: 0 -> 0; matrix products, arithmetic and copies ran while one was open for 0% -> 0% of each run, Pallas kernels for 2% -> 3%
where the time goes in v3:
time: 72.7 us; the launch traced here: 72.4 us
  blocking collectives  40.4 us (56%)
  starting transfers between devices  25.3 us (35%)
  Pallas kernels  4.52 us (6%)
  local copies, waits for them, and re-layouts  1.44 us (2%)
    all_to_all x1, blocking collectives, body(): lax.all_to_all(panel.reshape(groups, 2 * own, DH), seq, 0, 0, tiled=True)  24.5 us
    all_to_all x1, starting transfers between devices, body(): lax.all_to_all(jnp.broadcast_to(keys_values[None], (groups, 2, own, DH)),...  18.8 us
    all_gather x1, blocking collectives, body(): lax.all_gather(out_grad, 'my', axis=0)  15.9 us
    ppermute x1, starting transfers between devices, body(): og_other = lax.ppermute(og, 'mc', [(0, 1), (1, 0)])  6.43 us
    pallas_call x1, Pallas kernels, body(): pl.pallas_call(lambda *refs: before_kernel(*refs, own=own), name='softmax...  2.23 us
    pallas_call x1, Pallas kernels, body(): pl.pallas_call(after_kernel, name='gradients', out_shape=(jax.ShapeDtypeS...  1.66 us
  transfers between devices with their start and end apart: 2, of which 0 were waited for; matrix products, arithmetic and copies ran while one was open for 0% of the time, Pallas kernels for 3%

profile of v3, /device:TPU:1, one launch (start us, length us, event | category | flops | bytes accessed | tf_op | source)
XLA Modules:
  0.0 72.4 jit_solution(17427527418193117392)
XLA Ops:
  0.6 1.4 %broadcast_in_dim.2 = bf16[48,2,2,256]{3,2,1,0:T(2,128)(2,1)} broadcast(bf16[2,2,256]{2,1,0:T(2,128)(2,1)} %param.7), dimensions={1,2,3} | broadcast | bytes 100352 | tf_op jit(solution)/shard_map/broadcast_in_dim | solution.py:114
  2.0 18.8 %all-to-all-start = ((bf16[48,2,2,256]{3,2,1,0:T(2,128)(2,1)}), bf16[48,2,2,256]{3,2,1,0:T(2,128)(2,1)S(1)}, u32[]{:S(2)}, u32[]{:S(2)}) async-start(bf16[48,2,2,256]{3,2,1,0:T(2,128)(2,1)} %broadcast_in_dim.2), calls=%async_computation | async-start | bytes 196608 | tf_op jit(solution)/shard_map/all_to_all | solution.py:113
  20.8 15.9 %all-gather = bf16[512,512]{1,0:T(8,128)(2,1)S(1)} all-gather(bf16[128,512]{1,0:T(8,128)(2,1)} %param.8), channel_id=2, replica_groups=mesh['sec'=2,'sx'=4,'sz'=12,'my'=4,'mc'=2] {'my'}, dimensions={0}, use_global_device_ids=true | all-gather | bytes 655360 | tf_op jit(solution)/shard_map/all_gather | solution.py:116
  36.8 0.0 all-to-all-done
  36.8 6.4 %collective-permute-start = (bf16[4,128,512]{2,1,0:T(8,128)(2,1)S(1)}, bf16[4,128,512]{2,1,0:T(8,128)(2,1)S(1)}, u32[]{:S(2)}, u32[]{:S(2)}) collective-permute-start(bf16[4,128,512]{2,1,0:T(8,128)(2,1)S(1)} %bitcast.1), channel_id=1, source_target_pairs={{0,1},{1,0},{2,3},{3,2},{4,5},{5,4},{6,7},{7,6},{8,9},{9,8},{10,11... | collective-permute-start | bytes 1572872 | tf_op jit(solution)/shard_map/ppermute | solution.py:117
  43.3 2.2 %softmax_and_own_columns.1 = (bf16[256,4096]{1,0:T(8,128)(2,1)S(1)}, bf16[128,256]{1,0:T(8,128)(2,1)S(1)}, f32[128,256]{1,0:T(8,128)S(1)}, f32[128,256]{1,0:T(8,...) custom-call(s32[2]{0:T(128)} %refs_0_.1, s32[2]{0:T(128)} %refs_1_.1, ...), custom_call_target="tpu_custom_call" | custom-call | tf_op jit(solution)/shard_map/softmax_and_own_columns/pallas_call | solution.py:118
  45.5 0.0 collective-permute-done.og_ref
  45.5 1.7 %gradients.1 = (bf16[128,256]{1,0:T(8,128)(2,1)}, bf16[192,256]{1,0:T(8,128)(2,1)S(1)}) custom-call(bf16[4,128,512]{2,1,0:T(8,128)(2,1)S(1)} %collective-permute-done.og_ref, bf16[192,256]{1,0:T(8,128)(2,1)S(1)} %reshape.11.refs_5_.kv_ref, bf16[256,4096]{1,0:T(8,128)(2,1)S(1)} %get-tuple-element.15.w_ref, bf16[128,256]{1,0:T(8,128)(2,1)S(1)} %get-tuple-element.16.q_ref, ...), custom_call_target="tpu_custom_call" | custom-call | tf_op jit(solution)/shard_map/gradients/pallas_call | solution.py:139
  47.2 24.5 %all_to_all.10.parts_ref = bf16[48,4,256]{2,1,0:T(4,128)(2,1)S(1)} all-to-all(bf16[48,4,256]{2,1,0:T(4,128)(2,1)S(1)} %reshape.12), channel_id=1, replica_groups=mesh['sec'=2,'sx'=4,'sz'=12,'my'=4,'mc'=2] {'sx','sz'}, dimensions={0} | all-to-all | bytes 196608 | tf_op jit(solution)/shard_map/all_to_all | solution.py:150
  71.7 0.6 sum_of_parts.1
  (2 shorter events, 0.1 us)
Async XLA Ops:
  2.0 34.8 %all-to-all-start = ((bf16[48,2,2,256]{3,2,1,0:T(2,128)(2,1)}), bf16[48,2,2,256]{3,2,1,0:T(2,128)(2,1)S(1)}, u32[]{:S(2)}, u32[]{:S(2)}) async-start(bf16[48,2,2,256]{3,2,1,0:T(2,128)(2,1)} %broadcast_in_dim.2), calls=%async_computation | async-start | bytes 196608 | tf_op jit(solution)/shard_map/all_to_all | solution.py:113
  36.8 8.7 %collective-permute-start = (bf16[4,128,512]{2,1,0:T(8,128)(2,1)S(1)}, bf16[4,128,512]{2,1,0:T(8,128)(2,1)S(1)}, u32[]{:S(2)}, u32[]{:S(2)}) collective-permute-start(bf16[4,128,512]{2,1,0:T(8,128)(2,1)S(1)} %bitcast.1), channel_id=1, source_target_pairs={{0,1},{1,0},{2,3},{3,2},{4,5},{5,4},{6,7},{7,6},{8,9},{9,8},{10,11... | collective-permute-start | bytes 1572872 | tf_op jit(solution)/shard_map/ppermute | solution.py:117

commit v4 on v3

v4 whole, which is shorter than its diff:
```python
import jax
import jax.numpy as jnp
from jax import lax
from jax.experimental import pallas as pl
from jax.experimental.pallas import tpu as pltpu
from jax.sharding import Mesh, PartitionSpec as P

DH = 256
F32 = jnp.float32
BF16 = jnp.bfloat16
VMEM = pl.BlockSpec(memory_space=pltpu.VMEM)
HBM = pl.BlockSpec(memory_space=pltpu.HBM)
PARAMS = pltpu.CompilerParams(vmem_limit_bytes=32 * 1024 * 1024)
KV_FIRST = 24
SUM_FIRST = 30


def dot_nt(a, b):
    return lax.dot_general(a, b, (((1,), (1,)), ((), ())), preferred_element_type=F32)


def dot_tn(a, b):
    return lax.dot_general(a, b, (((0,), (0,)), ((), ())), preferred_element_type=F32)


def masked_softmax(scores, allowed):
    scores = jnp.where(allowed, scores, -1e30)
    expo = jnp.where(allowed, jnp.exp(scores - jnp.max(scores, axis=1, keepdims=True)), 0.0)
    return expo / jnp.sum(expo, axis=1, keepdims=True)


def project(og_ref, w_ref, core):
    chips, rows, slab = og_ref.shape
    total = jnp.zeros((rows, DH), F32)
    for chip in range(chips):
        first = pl.multiple_of((2 * chip + core) * slab, slab)
        total += dot_nt(og_ref[chip], w_ref[:, pl.ds(first, slab)])
    return total


def swap_keys_values(kv, own):
    total = kv.shape[0]
    r = lax.broadcasted_iota(jnp.int32, (total, total), 0)
    c = lax.broadcasted_iota(jnp.int32, (total, total), 1)
    partner = jnp.where((r % (2 * own)) < own, r + own, r - own)
    swap = jnp.where(c == partner, 1.0, 0.0).astype(BF16)
    return jnp.dot(swap, kv, preferred_element_type=F32).astype(BF16)


def probabilities(q, kv, swapped, enc_limit, own):
    rows, total = q.shape[0], kv.shape[0]
    peers = total // (2 * own)
    scale = DH ** (-0.5)
    col = lax.broadcasted_iota(jnp.int32, (rows, total), 1)
    is_key = (col % (2 * own)) < own
    peer = (col // (2 * own) + KV_FIRST) % peers
    inside = peer * own + col % own < enc_limit
    at_keys = masked_softmax(dot_nt(q, kv) * scale, is_key & inside)
    at_values = masked_softmax(dot_nt(q, swapped) * scale, jnp.logical_not(is_key) & inside)
    return at_keys, at_values.astype(BF16)


def gradients(g, q, kv, swapped, prob, prob_v, dq_ref, panel_ref, own):
    scale = DH ** (-0.5)
    grad_prob = dot_nt(g, swapped)
    delta = jnp.sum(prob * grad_prob, axis=1, keepdims=True)
    grad_score = (prob * (grad_prob - delta)).astype(BF16)
    panel = dot_tn(grad_score, q) * scale + dot_tn(prob_v, g)
    peers = panel.shape[0] // (2 * own)
    shift = ((SUM_FIRST - KV_FIRST) % peers) * 2 * own
    if shift:
        panel = jnp.concatenate([panel[shift:], panel[:shift]], axis=0)
    panel_ref[...] = panel.astype(BF16)
    dq_ref[...] = (jnp.dot(grad_score, kv, preferred_element_type=F32) * scale).astype(BF16)


def sum_kernel(parts_ref, out_ref):
    total = jnp.sum(parts_ref[...].astype(F32), axis=0).astype(BF16)
    own = out_ref.shape[1]
    out_ref[0] = total[:own]
    out_ref[1] = total[own:]


def in_hbm(x):
    return pltpu.with_memory_space_constraint(x, pltpu.HBM)


def exchange(x, first):
    peers = x.shape[0]
    order = [(first + i) % peers for i in range(peers)]
    return lax.all_to_all(x, "seq", 0, 0, tiled=True, axis_index_groups=[order])


def sum_over_seq(panel, groups, own):
    parts = exchange(panel.reshape(groups, 2 * own, DH), SUM_FIRST)
    return pl.pallas_call(
        sum_kernel,
        name="sum_of_parts",
        out_shape=jax.ShapeDtypeStruct((2, own, DH), BF16),
        in_specs=[VMEM],
        out_specs=VMEM,
        compiler_params=PARAMS,
    )(parts)


def start_copies(pairs, sems):
    copies = [pltpu.make_async_copy(src, dst, sems.at[i]) for i, (src, dst) in enumerate(pairs)]
    for copy in copies:
        copy.start()
    return copies


def before_kernel(
    enc_hbm, dec_hbm, w_hbm, q_hbm, og_ref, kv_ref,
    w_ref, q_ref, part_ref, mask_ref, pk_ref, pv_ref, sw_ref,
    enc_ref, dec_ref, sems, *, own,
):
    copies = start_copies(
        ((enc_hbm, enc_ref), (dec_hbm, dec_ref), (q_hbm, q_ref), (w_hbm, w_ref)), sems
    )
    rows = q_ref.shape[0]
    sec = lax.axis_index("sec")
    kv = kv_ref[...]
    swapped = swap_keys_values(kv, own)
    sw_ref[...] = swapped
    for copy in copies[:3]:
        copy.wait()
    pk_ref[...], pv_ref[...] = probabilities(q_ref[...], kv, swapped, enc_ref[sec], own)
    valid_rows = dec_ref[sec] - lax.axis_index("seq") * rows
    row = lax.broadcasted_iota(jnp.int32, (rows, DH), 0)
    mask_ref[...] = jnp.where(row < valid_rows, 1.0, 0.0)
    copies[3].wait()
    part_ref[...] = project(og_ref, w_ref, lax.axis_index("mc"))


def after_kernel(
    og_ref, kv_ref, w_ref, q_ref, part_ref, mask_ref, pk_ref, pv_ref, sw_ref, dq_ref, panel_ref, *, own
):
    grad = part_ref[...] + project(og_ref, w_ref, 1 - lax.axis_index("mc"))
    g = jnp.where(mask_ref[...] > 0.0, grad, 0.0).astype(BF16)
    gradients(
        g, q_ref[...], kv_ref[...], sw_ref[...], pk_ref[...], pv_ref[...], dq_ref, panel_ref, own
    )


def body(queries, keys_values, out_grad, out_weight, enc_len, dec_len):
    rows = queries.shape[0]
    own = keys_values.shape[1]
    groups = lax.axis_size("seq")
    total = 2 * own * groups
    kv = exchange(jnp.broadcast_to(keys_values[None], (groups, 2, own, DH)), KV_FIRST)
    kv = kv.reshape(total, DH)
    og, kv = lax.optimization_barrier((lax.all_gather(out_grad, "my", axis=0), kv))
    og_other = lax.ppermute(og, "mc", [(0, 1), (1, 0)])
    kept = pl.pallas_call(
        lambda *refs: before_kernel(*refs, own=own),
        name="softmax_and_own_columns",
        out_shape=(
            jax.ShapeDtypeStruct(out_weight.shape, BF16),
            jax.ShapeDtypeStruct((rows, DH), BF16),
            jax.ShapeDtypeStruct((rows, DH), F32),
            jax.ShapeDtypeStruct((rows, DH), F32),
            jax.ShapeDtypeStruct((rows, total), F32),
            jax.ShapeDtypeStruct((rows, total), BF16),
            jax.ShapeDtypeStruct((total, DH), BF16),
        ),
        in_specs=[HBM] * 4 + [VMEM] * 2,
        out_specs=(VMEM,) * 7,
        scratch_shapes=[
            pltpu.SMEM(enc_len.shape, jnp.int32),
            pltpu.SMEM(dec_len.shape, jnp.int32),
            pltpu.SemaphoreType.DMA((4,)),
        ],
        compiler_params=PARAMS,
    )(*map(in_hbm, (enc_len, dec_len, out_weight, queries)), og, kv)
    query_grad, panel = pl.pallas_call(
        lambda *refs: after_kernel(*refs, own=own),
        name="gradients",
        out_shape=(
            jax.ShapeDtypeStruct((rows, DH), BF16),
            jax.ShapeDtypeStruct((total, DH), BF16),
        ),
        in_specs=[VMEM] * 9,
        out_specs=(VMEM, VMEM),
        compiler_params=PARAMS,
    )(og_other, kv, *kept)
    return query_grad, sum_over_seq(panel, groups, own)


def solution(mesh):
    sizes = dict(mesh.shape)
    fine = Mesh(
        mesh.devices.reshape(sizes["sec"], sizes["seq"], sizes["mp"] // 2, 2),
        ("sec", "seq", "my", "mc"),
    )
    tok, mp = ("sec", "seq"), ("my", "mc")
    return jax.shard_map(
        body,
        mesh=fine,
        in_specs=(P(tok, mp), P(None, tok, mp), P(tok, mp), P(mp, None), P(), P()),
        out_specs=(P(tok, mp), P(None, tok, mp)),
        check_vma=False,
    )
```

time: 72.7 us -> 65 us (0.89)
  blocking collectives: 40.4 us -> 31.6 us
  starting transfers between devices: 25.3 us -> 26.5 us
    all_to_all x1, blocking collectives: 24.5 us -> 15.8 us  [exchange(): return lax.all_to_all(x, 'seq', 0, 0, tiled=True, axis_index_groups=[order])]
where the time goes in v4:
time: 65 us; the launch traced here: 64.7 us
  blocking collectives  31.6 us (49%)
  starting transfers between devices  26.5 us (41%)
  Pallas kernels  4.52 us (7%)
  local copies, waits for them, and re-layouts  1.44 us (2%)
  between operations  0.67 us (1%)
    all_to_all x1, starting transfers between devices, exchange(): return lax.all_to_all(x, 'seq', 0, 0, tiled=True, axis_index_groups=[order])  19.5 us
    all_gather x1, blocking collectives, body(): lax.all_gather(out_grad, 'my', axis=0)  15.8 us
    all_to_all x1, blocking collectives, exchange(): return lax.all_to_all(x, 'seq', 0, 0, tiled=True, axis_index_groups=[order])  15.8 us
    ppermute x1, starting transfers between devices, body(): og_other = lax.ppermute(og, 'mc', [(0, 1), (1, 0)])  7.01 us
    pallas_call x1, Pallas kernels, body(): pl.pallas_call(lambda *refs: before_kernel(*refs, own=own), name='softmax...  2.22 us
    pallas_call x1, Pallas kernels, body(): pl.pallas_call(lambda *refs: after_kernel(*refs, own=own), name='gradient...  1.66 us
    broadcast_in_dim x1, local copies, waits for them, and re-layouts, body(): jnp.broadcast_to(keys_values[None], (groups, 2, own, DH))  1.37 us
  transfers between devices with their start and end apart: 2, of which 0 were waited for; matrix products, arithmetic and copies ran while one was open for 0% of the time, Pallas kernels for 3%

profile of v4, /device:TPU:1, one launch (start us, length us, event | category | flops | bytes accessed | tf_op | source)
XLA Modules:
  0.0 64.7 jit_solution(11528356248903108932)
XLA Ops:
  0.6 1.4 %broadcast_in_dim.2 = bf16[48,2,2,256]{3,2,1,0:T(2,128)(2,1)} broadcast(bf16[2,2,256]{2,1,0:T(2,128)(2,1)} %param.7), dimensions={1,2,3} | broadcast | bytes 100352 | tf_op jit(solution)/shard_map/broadcast_in_dim | solution.py:151
  2.0 19.5 %all-to-all-start = ((bf16[48,2,2,256]{3,2,1,0:T(2,128)(2,1)}), bf16[48,2,2,256]{3,2,1,0:T(2,128)(2,1)S(1)}, u32[]{:S(2)}, u32[]{:S(2)}) async-start(bf16[48,2,2,256]{3,2,1,0:T(2,128)(2,1)} %broadcast_in_dim.2), calls=%async_computation | async-start | bytes 196608 | tf_op jit(solution)/shard_map/all_to_all | solution.py:91
  21.5 15.8 %all-gather = bf16[512,512]{1,0:T(8,128)(2,1)S(1)} all-gather(bf16[128,512]{1,0:T(8,128)(2,1)} %param.8), channel_id=2, replica_groups=mesh['sec'=2,'seq'=48,'my'=4,'mc'=2] {'my'}, dimensions={0}, use_global_device_ids=true | all-gather | bytes 655360 | tf_op jit(solution)/shard_map/all_gather | solution.py:153
  37.3 0.0 all-to-all-done
  37.3 7.0 %collective-permute-start = (bf16[4,128,512]{2,1,0:T(8,128)(2,1)S(1)}, bf16[4,128,512]{2,1,0:T(8,128)(2,1)S(1)}, u32[]{:S(2)}, u32[]{:S(2)}) collective-permute-start(bf16[4,128,512]{2,1,0:T(8,128)(2,1)S(1)} %bitcast.1), channel_id=1, source_target_pairs={{0,1},{1,0},{2,3},{3,2},{4,5},{5,4},{6,7},{7,6},{8,9},{9,8},{10,11... | collective-permute-start | bytes 1572872 | tf_op jit(solution)/shard_map/ppermute | solution.py:154
  44.4 2.2 %softmax_and_own_columns.1 = (bf16[256,4096]{1,0:T(8,128)(2,1)S(1)}, bf16[128,256]{1,0:T(8,128)(2,1)S(1)}, f32[128,256]{1,0:T(8,128)S(1)}, f32[128,256]{1,0:T(8,...) custom-call(s32[2]{0:T(128)} %refs_0_.1, s32[2]{0:T(128)} %refs_1_.1, ...), custom_call_target="tpu_custom_call" | custom-call | tf_op jit(solution)/shard_map/softmax_and_own_columns/pallas_call | solution.py:155
  46.6 0.0 collective-permute-done.refs_0_
  46.6 1.7 %gradients.1 = (bf16[128,256]{1,0:T(8,128)(2,1)}, bf16[192,256]{1,0:T(8,128)(2,1)S(1)}) custom-call(bf16[4,128,512]{2,1,0:T(8,128)(2,1)S(1)} %collective-permute-done.refs_0_, bf16[192,256]{1,0:T(8,128)(2,1)S(1)} %reshape.11.refs_5_.refs_1_, bf16[256,4096]{1,0:T(8,128)(2,1)S(1)} %get-tuple-element.15.refs_2_, ...), custom_call_target="tpu_custom_call" | custom-call | tf_op jit(solution)/shard_map/gradients/pallas_call | solution.py:176
  48.3 15.8 %all_to_all.10.parts_ref = bf16[48,4,256]{2,1,0:T(4,128)(2,1)S(1)} all-to-all(bf16[48,4,256]{2,1,0:T(4,128)(2,1)S(1)} %reshape.12), channel_id=1, replica_groups={{240,248,256,264,272,280,288,296,304,312,320,328,336,344,352,360,368,37..., dimensions={0} | all-to-all | bytes 196608 | tf_op jit(solution)/shard_map/all_to_all | solution.py:91
  64.1 0.6 sum_of_parts.1
  (2 shorter events, 0.1 us)
Async XLA Ops:
  2.0 35.3 %all-to-all-start = ((bf16[48,2,2,256]{3,2,1,0:T(2,128)(2,1)}), bf16[48,2,2,256]{3,2,1,0:T(2,128)(2,1)S(1)}, u32[]{:S(2)}, u32[]{:S(2)}) async-start(bf16[48,2,2,256]{3,2,1,0:T(2,128)(2,1)} %broadcast_in_dim.2), calls=%async_computation | async-start | bytes 196608 | tf_op jit(solution)/shard_map/all_to_all | solution.py:91
  37.3 9.3 %collective-permute-start = (bf16[4,128,512]{2,1,0:T(8,128)(2,1)S(1)}, bf16[4,128,512]{2,1,0:T(8,128)(2,1)S(1)}, u32[]{:S(2)}, u32[]{:S(2)}) collective-permute-start(bf16[4,128,512]{2,1,0:T(8,128)(2,1)S(1)} %bitcast.1), channel_id=1, source_target_pairs={{0,1},{1,0},{2,3},{3,2},{4,5},{5,4},{6,7},{7,6},{8,9},{9,8},{10,11... | collective-permute-start | bytes 1572872 | tf_op jit(solution)/shard_map/ppermute | solution.py:154

commit v5 on v4

--- a/solution.py
+++ b/solution.py
@@ -13,6 +13,7 @@
 PARAMS = pltpu.CompilerParams(vmem_limit_bytes=32 * 1024 * 1024)
 KV_FIRST = 24
 SUM_FIRST = 30
+CHIP_FIRST = 0
 
 
 def dot_nt(a, b):
@@ -33,21 +34,20 @@
     chips, rows, slab = og_ref.shape
     total = jnp.zeros((rows, DH), F32)
     for chip in range(chips):
-        first = pl.multiple_of((2 * chip + core) * slab, slab)
+        holder = (chip + CHIP_FIRST) % chips
+        first = pl.multiple_of((2 * holder + core) * slab, slab)
         total += dot_nt(og_ref[chip], w_ref[:, pl.ds(first, slab)])
     return total
 
 
-def swap_keys_values(kv, own):
-    total = kv.shape[0]
+def swap_matrix(total, own):
     r = lax.broadcasted_iota(jnp.int32, (total, total), 0)
     c = lax.broadcasted_iota(jnp.int32, (total, total), 1)
     partner = jnp.where((r % (2 * own)) < own, r + own, r - own)
-    swap = jnp.where(c == partner, 1.0, 0.0).astype(BF16)
-    return jnp.dot(swap, kv, preferred_element_type=F32).astype(BF16)
-
-
-def probabilities(q, kv, swapped, enc_limit, own):
+    return jnp.where(c == partner, 1.0, 0.0).astype(BF16)
+
+
+def probabilities(q, kv, swap, enc_limit, own):
     rows, total = q.shape[0], kv.shape[0]
     peers = total // (2 * own)
     scale = DH ** (-0.5)
@@ -56,7 +56,7 @@
     peer = (col // (2 * own) + KV_FIRST) % peers
     inside = peer * own + col % own < enc_limit
     at_keys = masked_softmax(dot_nt(q, kv) * scale, is_key & inside)
-    at_values = masked_softmax(dot_nt(q, swapped) * scale, jnp.logical_not(is_key) & inside)
+    at_values = jnp.dot(at_keys.astype(BF16), swap, preferred_element_type=F32)
     return at_keys, at_values.astype(BF16)
 
 
@@ -91,6 +91,40 @@
     return lax.all_to_all(x, "seq", 0, 0, tiled=True, axis_index_groups=[order])
 
 
+def gather_chips(x):
+    chips = lax.axis_size("my")
+    order = [(CHIP_FIRST + i) % chips for i in range(chips)]
+    return lax.all_gather(x, "my", axis=0, axis_index_groups=[order])
+
+
+def opening_kernel(
+    enc_hbm, dec_hbm, kv_hbm, w_hbm, q_hbm, copies_hbm, w_ref, q_ref, mask_ref, limit_ref,
+    enc_ref, dec_ref, kv_ref, copies_ref, sems,
+):
+    copies = start_copies(
+        ((kv_hbm, kv_ref), (enc_hbm, enc_ref), (dec_hbm, dec_ref), (w_hbm, w_ref), (q_hbm, q_ref)),
+        sems,
+    )
+    own = kv_ref.shape[1]
+    copies[0].wait()
+    for half in range(2):
+        copies_ref[:, half * own : (half + 1) * own] = jnp.broadcast_to(
+            kv_ref[half][None], (copies_ref.shape[0], own, DH)
+        )
+    out = pltpu.make_async_copy(copies_ref, copies_hbm, sems.at[5])
+    out.start()
+    copies[1].wait()
+    copies[2].wait()
+    sec = lax.axis_index("sec")
+    limit_ref[...] = jnp.full(limit_ref.shape, enc_ref[sec], jnp.int32)
+    valid_rows = dec_ref[sec] - lax.axis_index("seq") * q_ref.shape[0]
+    row = lax.broadcasted_iota(jnp.int32, mask_ref.shape, 0)
+    mask_ref[...] = jnp.where(row < valid_rows, 1.0, 0.0)
+    copies[3].wait()
+    copies[4].wait()
+    out.wait()
+
+
 def sum_over_seq(panel, groups, own):
     parts = exchange(panel.reshape(groups, 2 * own, DH), SUM_FIRST)
     return pl.pallas_call(
@@ -111,30 +145,17 @@
 
 
 def before_kernel(
-    enc_hbm, dec_hbm, w_hbm, q_hbm, og_ref, kv_ref,
-    w_ref, q_ref, part_ref, mask_ref, pk_ref, pv_ref, sw_ref,
-    enc_ref, dec_ref, sems, *, own,
+    limit_ref, w_ref, q_ref, og_ref, kv_ref, part_ref, pk_ref, pv_ref, sw_ref, *, own
 ):
-    copies = start_copies(
-        ((enc_hbm, enc_ref), (dec_hbm, dec_ref), (q_hbm, q_ref), (w_hbm, w_ref)), sems
-    )
-    rows = q_ref.shape[0]
-    sec = lax.axis_index("sec")
     kv = kv_ref[...]
-    swapped = swap_keys_values(kv, own)
-    sw_ref[...] = swapped
-    for copy in copies[:3]:
-        copy.wait()
-    pk_ref[...], pv_ref[...] = probabilities(q_ref[...], kv, swapped, enc_ref[sec], own)
-    valid_rows = dec_ref[sec] - lax.axis_index("seq") * rows
-    row = lax.broadcasted_iota(jnp.int32, (rows, DH), 0)
-    mask_ref[...] = jnp.where(row < valid_rows, 1.0, 0.0)
-    copies[3].wait()
+    swap = swap_matrix(kv.shape[0], own)
+    pk_ref[...], pv_ref[...] = probabilities(q_ref[...], kv, swap, limit_ref[0:1, 0:1], own)
+    sw_ref[...] = jnp.dot(swap, kv, preferred_element_type=F32).astype(BF16)
     part_ref[...] = project(og_ref, w_ref, lax.axis_index("mc"))
 
 
 def after_kernel(
-    og_ref, kv_ref, w_ref, q_ref, part_ref, mask_ref, pk_ref, pv_ref, sw_ref, dq_ref, panel_ref, *, own
+    og_ref, kv_ref, w_ref, q_ref, mask_ref, part_ref, pk_ref, pv_ref, sw_ref, dq_ref, panel_ref, *, own
 ):
     grad = part_ref[...] + project(og_ref, w_ref, 1 - lax.axis_index("mc"))
     g = jnp.where(mask_ref[...] > 0.0, grad, 0.0).astype(BF16)
@@ -148,31 +169,44 @@
     own = keys_values.shape[1]
     groups = lax.axis_size("seq")
     total = 2 * own * groups
-    kv = exchange(jnp.broadcast_to(keys_values[None], (groups, 2, own, DH)), KV_FIRST)
+    copies, w, q, mask, limit = pl.pallas_call(
+        opening_kernel,
+        name="kv_copies_and_loads",
+        out_shape=(
+            jax.ShapeDtypeStruct((groups, 2 * own, DH), BF16),
+            jax.ShapeDtypeStruct(out_weight.shape, BF16),
+            jax.ShapeDtypeStruct((rows, DH), BF16),
+            jax.ShapeDtypeStruct((rows, DH), F32),
+            jax.ShapeDtypeStruct((8, 128), jnp.int32),
+        ),
+        in_specs=[HBM] * 5,
+        out_specs=(HBM,) + (VMEM,) * 4,
+        scratch_shapes=[
+            pltpu.SMEM(enc_len.shape, jnp.int32),
+            pltpu.SMEM(dec_len.shape, jnp.int32),
+            pltpu.VMEM(keys_values.shape, BF16),
+            pltpu.VMEM((groups, 2 * own, DH), BF16),
+            pltpu.SemaphoreType.DMA((6,)),
+        ],
+        compiler_params=PARAMS,
+    )(*map(in_hbm, (enc_len, dec_len, keys_values, out_weight, queries)))
+    kv = exchange(copies, KV_FIRST)
     kv = kv.reshape(total, DH)
-    og, kv = lax.optimization_barrier((lax.all_gather(out_grad, "my", axis=0), kv))
+    og, kv = lax.optimization_barrier((gather_chips(out_grad), kv))
     og_other = lax.ppermute(og, "mc", [(0, 1), (1, 0)])
     kept = pl.pallas_call(
         lambda *refs: before_kernel(*refs, own=own),
         name="softmax_and_own_columns",
         out_shape=(
-            jax.ShapeDtypeStruct(out_weight.shape, BF16),
-            jax.ShapeDtypeStruct((rows, DH), BF16),
-            jax.ShapeDtypeStruct((rows, DH), F32),
             jax.ShapeDtypeStruct((rows, DH), F32),
             jax.ShapeDtypeStruct((rows, total), F32),
             jax.ShapeDtypeStruct((rows, total), BF16),
             jax.ShapeDtypeStruct((total, DH), BF16),
         ),
-        in_specs=[HBM] * 4 + [VMEM] * 2,
-        out_specs=(VMEM,) * 7,
-        scratch_shapes=[
-            pltpu.SMEM(enc_len.shape, jnp.int32),
-            pltpu.SMEM(dec_len.shape, jnp.int32),
-            pltpu.SemaphoreType.DMA((4,)),
-        ],
-        compiler_params=PARAMS,
-    )(*map(in_hbm, (enc_len, dec_len, out_weight, queries)), og, kv)
+        in_specs=[VMEM] * 5,
+        out_specs=(VMEM,) * 4,
+        compiler_params=PARAMS,
+    )(limit, w, q, og, kv)
     query_grad, panel = pl.pallas_call(
         lambda *refs: after_kernel(*refs, own=own),
         name="gradients",
@@ -183,7 +217,7 @@
         in_specs=[VMEM] * 9,
         out_specs=(VMEM, VMEM),
         compiler_params=PARAMS,
-    )(og_other, kv, *kept)
+    )(og_other, kv, w, q, mask, *kept)
     return query_grad, sum_over_seq(panel, groups, own)
 
 

time: 65 us -> 64.1 us (0.986)
  local copies, waits for them, and re-layouts: 1.44 us -> 0.06 us
  blocking collectives: 31.6 us -> 30.6 us
  waiting for transfers between devices: 0.01 us -> 0.69 us
    pallas_call x0 -> x1, Pallas kernels: none -> 1.7 us  [body(): pl.pallas_call(opening_kernel, name='kv_copies_and_loads', out_shape=(jax...]
    pallas_call x1, Pallas kernels: 2.22 us -> 0.82 us  [body(): pl.pallas_call(lambda *refs: before_kernel(*refs, own=own), name='softmax...]
    broadcast_in_dim x1 -> x0, local copies, waits for them, and re-layouts: 1.37 us -> none  [body(): jnp.broadcast_to(keys_values[None], (groups, 2, own, DH))]
    all_to_all x1, blocking collectives: 15.8 us -> 15 us  [exchange(): return lax.all_to_all(x, 'seq', 0, 0, tiled=True, axis_index_groups=[order])]
    ppermute x1, waiting for transfers between devices: 0.01 us -> 0.69 us  [body(): og_other = lax.ppermute(og, 'mc', [(0, 1), (1, 0)])]
  transfers between devices with their start and end apart: 2 -> 2, of which waited for: 0 -> 1; matrix products, arithmetic and copies ran while one was open for 0% -> 0% of each run, Pallas kernels for 3% -> 1%
where the time goes in v5:
time: 64.1 us; the launch traced here: 63.4 us
  blocking collectives  30.6 us (48%)
  starting transfers between devices  26.5 us (41%)
  Pallas kernels  4.81 us (8%)
  waiting for transfers between devices  0.69 us (1%)
  between operations  0.68 us (1%)
    all_to_all x1, starting transfers between devices, exchange(): return lax.all_to_all(x, 'seq', 0, 0, tiled=True, axis_index_groups=[order])  19.5 us
    all_gather x1, blocking collectives, gather_chips(): return lax.all_gather(x, 'my', axis=0, axis_index_groups=[order])  15.6 us
    all_to_all x1, blocking collectives, exchange(): return lax.all_to_all(x, 'seq', 0, 0, tiled=True, axis_index_groups=[order])  15 us
    ppermute x1, starting transfers between devices, body(): og_other = lax.ppermute(og, 'mc', [(0, 1), (1, 0)])  7.01 us
    pallas_call x1, Pallas kernels, body(): pl.pallas_call(opening_kernel, name='kv_copies_and_loads', out_shape=(jax...  1.7 us
    pallas_call x1, Pallas kernels, body(): pl.pallas_call(lambda *refs: after_kernel(*refs, own=own), name='gradient...  1.65 us
  transfers between devices with their start and end apart: 2, of which 1 were waited for; matrix products, arithmetic and copies ran while one was open for 0% of the time, Pallas kernels for 1%

profile of v5, /device:TPU:1, one launch (start us, length us, event | category | flops | bytes accessed | tf_op | source)
XLA Modules:
  0.0 63.4 jit_solution(12872425388582408567)
XLA Ops:
  0.6 0.0 copy-start
  0.6 1.7 %kv_copies_and_loads.1 = (bf16[48,4,256]{2,1,0:T(4,128)(2,1)}, bf16[256,4096]{1,0:T(8,128)(2,1)S(1)}, bf16[128,256]{1,0:T(8,128)(2,1)S(1)}, f32[128,256]{1,0:T(8,128)S(1)}, s32[8,128]{1,0:T(8,128)S(1)}) custom-call(s32[2]{0:T(128)} %enc_hbm.1, s32[2]{0:T(128)} %dec_hbm.1, bf16[2,2,256]{2,1,0:T(2,128)(2,1)} %kv_hbm.1, bf16[256,4096]{1,0:T(8,128)(2,1)} %w_hbm.1, ...), custom_call_target="tpu_custom_call" | custom-call | tf_op jit(solution)/shard_map/kv_copies_and_loads/pallas_call | solution.py:172
  2.3 19.5 %all-to-all-start = ((bf16[48,4,256]{2,1,0:T(4,128)(2,1)}), bf16[48,4,256]{2,1,0:T(4,128)(2,1)S(1)}, u32[]{:S(2)}, u32[]{:S(2)}) async-start(bf16[48,4,256]{2,1,0:T(4,128)(2,1)} %get-tuple-element.15), calls=%async_computation | async-start | bytes 196608 | tf_op jit(solution)/shard_map/all_to_all | solution.py:91
  21.8 0.0 copy-done
  21.8 15.6 %all-gather = bf16[512,512]{1,0:T(8,128)(2,1)S(1)} all-gather(bf16[128,512]{1,0:T(8,128)(2,1)S(1)} %copy-done), channel_id=2, replica_groups={{0,2,4,6},{1,3,5,7},{8,10,12,14},{9,11,13,15},{16,18,20,22},{17,19,21,2..., dimensions={0}, use_global_device_ids=true | all-gather | bytes 655360 | tf_op jit(solution)/shard_map/all_gather | solution.py:97
  37.4 0.0 all-to-all-done
  37.5 7.0 %collective-permute-start = (bf16[4,128,512]{2,1,0:T(8,128)(2,1)S(1)}, bf16[4,128,512]{2,1,0:T(8,128)(2,1)S(1)}, u32[]{:S(2)}, u32[]{:S(2)}) collective-permute-start(bf16[4,128,512]{2,1,0:T(8,128)(2,1)S(1)} %bitcast.1), channel_id=1, source_target_pairs={{0,1},{1,0},{2,3},{3,2},{4,5},{5,4},{6,7},{7,6},{8,9},{9,8},{10,11... | collective-permute-start | bytes 1572872 | tf_op jit(solution)/shard_map/ppermute | solution.py:196
  44.5 0.8 %softmax_and_own_columns.1 = (f32[128,256]{1,0:T(8,128)S(1)}, f32[128,192]{1,0:T(8,128)S(1)}, bf16[128,192]{1,0:T(8,128)(2,1)S(1)}, bf16[192,256]{1,0:T(8,128)(2,1)S(1)}) custom-call(s32[8,128]{1,0:T(8,128)S(1)} %get-tuple-element.21.refs_0_, bf16[256,4096]{1,0:T(8,128)(2,1)S(1)} %get-tuple-element.18.refs_1_.refs_2_, ...), custom_call_target="tpu_custom_call" | custom-call | tf_op jit(solution)/shard_map/softmax_and_own_columns/pallas_call | solution.py:197
  45.3 0.7 %collective-permute-done.refs_0_ = bf16[4,128,512]{2,1,0:T(8,128)(2,1)S(1)} collective-permute-done((bf16[4,128,512]{2,1,0:T(8,128)(2,1)S(1)}, bf16[4,128,512]{2,1,0:T(8,128)(2,1)S(1)}, u32[]{:S(2)}, u32[]{:S(2)}) %collective-permute-start) | collective-permute-done | bytes 524320 | tf_op jit(solution)/shard_map/ppermute | solution.py:196
  46.0 1.6 %gradients.1 = (bf16[128,256]{1,0:T(8,128)(2,1)}, bf16[192,256]{1,0:T(8,128)(2,1)S(1)}) custom-call(bf16[4,128,512]{2,1,0:T(8,128)(2,1)S(1)} %collective-permute-done.refs_0_, bf16[192,256]{1,0:T(8,128)(2,1)S(1)} %reshape.10.refs_4_.refs_1_, bf16[256,4096]{1,0:T(8,128)(2,1)S(1)} %get-tuple-element.18.refs_1_.refs_2_, ...), custom_call_target="tpu_custom_call" | custom-call | tf_op jit(solution)/shard_map/gradients/pallas_call | solution.py:210
  47.7 15.0 %all_to_all.10.parts_ref = bf16[48,4,256]{2,1,0:T(4,128)(2,1)S(1)} all-to-all(bf16[48,4,256]{2,1,0:T(4,128)(2,1)S(1)} %reshape.11), channel_id=1, replica_groups={{240,248,256,264,272,280,288,296,304,312,320,328,336,344,352,360,368,37..., dimensions={0} | all-to-all | bytes 196608 | tf_op jit(solution)/shard_map/all_to_all | solution.py:91
  62.7 0.6 %sum_of_parts.1 = bf16[2,2,256]{2,1,0:T(2,128)(2,1)} custom-call(bf16[48,4,256]{2,1,0:T(4,128)(2,1)S(1)} %all_to_all.10.parts_ref), custom_call_target="tpu_custom_call" | custom-call | tf_op jit(solution)/shard_map/sum_of_parts/pallas_call | solution.py:130
  (2 shorter events, 0.1 us)
Async XLA Ops:
  0.6 21.2 %copy-start = (bf16[128,512]{1,0:T(8,128)(2,1)S(1)}, bf16[128,512]{1,0:T(8,128)(2,1)}, u32[]{:S(2)}) copy-start(bf16[128,512]{1,0:T(8,128)(2,1)} %param.8) | copy-start | bytes 393220
  2.3 35.1 %all-to-all-start = ((bf16[48,4,256]{2,1,0:T(4,128)(2,1)}), bf16[48,4,256]{2,1,0:T(4,128)(2,1)S(1)}, u32[]{:S(2)}, u32[]{:S(2)}) async-start(bf16[48,4,256]{2,1,0:T(4,128)(2,1)} %get-tuple-element.15), calls=%async_computation | async-start | bytes 196608 | tf_op jit(solution)/shard_map/all_to_all | solution.py:91
  37.5 8.5 %collective-permute-start = (bf16[4,128,512]{2,1,0:T(8,128)(2,1)S(1)}, bf16[4,128,512]{2,1,0:T(8,128)(2,1)S(1)}, u32[]{:S(2)}, u32[]{:S(2)}) collective-permute-start(bf16[4,128,512]{2,1,0:T(8,128)(2,1)S(1)} %bitcast.1), channel_id=1, source_target_pairs={{0,1},{1,0},{2,3},{3,2},{4,5},{5,4},{6,7},{7,6},{8,9},{9,8},{10,11... | collective-permute-start | bytes 1572872 | tf_op jit(solution)/shard_map/ppermute | solution.py:196

commit v6 on v5

--- a/solution.py
+++ b/solution.py
@@ -53,7 +53,7 @@
     scale = DH ** (-0.5)
     col = lax.broadcasted_iota(jnp.int32, (rows, total), 1)
     is_key = (col % (2 * own)) < own
-    peer = (col // (2 * own) + KV_FIRST) % peers
+    peer = (KV_FIRST + peers - col // (2 * own)) % peers
     inside = peer * own + col % own < enc_limit
     at_keys = masked_softmax(dot_nt(q, kv) * scale, is_key & inside)
     at_values = jnp.dot(at_keys.astype(BF16), swap, preferred_element_type=F32)
@@ -67,7 +67,7 @@
     grad_score = (prob * (grad_prob - delta)).astype(BF16)
     panel = dot_tn(grad_score, q) * scale + dot_tn(prob_v, g)
     peers = panel.shape[0] // (2 * own)
-    shift = ((SUM_FIRST - KV_FIRST) % peers) * 2 * own
+    shift = ((KV_FIRST - SUM_FIRST) % peers) * 2 * own
     if shift:
         panel = jnp.concatenate([panel[shift:], panel[:shift]], axis=0)
     panel_ref[...] = panel.astype(BF16)
@@ -87,7 +87,7 @@
 
 def exchange(x, first):
     peers = x.shape[0]
-    order = [(first + i) % peers for i in range(peers)]
+    order = [(first - i) % peers for i in range(peers)]
     return lax.all_to_all(x, "seq", 0, 0, tiled=True, axis_index_groups=[order])
 
 

time: 64.1 us -> 63.9 us (level)
  no operation moved by 1% of the time
where the time goes in v6:
time: 63.9 us; the launch traced here: 63.3 us
  blocking collectives  30.6 us (48%)
  starting transfers between devices  26.5 us (41%)
  Pallas kernels  4.81 us (8%)
  waiting for transfers between devices  0.69 us (1%)
  between operations  0.68 us (1%)
    all_to_all x1, starting transfers between devices, exchange(): return lax.all_to_all(x, 'seq', 0, 0, tiled=True, axis_index_groups=[order])  19.5 us
    all_gather x1, blocking collectives, gather_chips(): return lax.all_gather(x, 'my', axis=0, axis_index_groups=[order])  15.6 us
    all_to_all x1, blocking collectives, exchange(): return lax.all_to_all(x, 'seq', 0, 0, tiled=True, axis_index_groups=[order])  15 us
    ppermute x1, starting transfers between devices, body(): og_other = lax.ppermute(og, 'mc', [(0, 1), (1, 0)])  7.01 us
    pallas_call x1, Pallas kernels, body(): pl.pallas_call(opening_kernel, name='kv_copies_and_loads', out_shape=(jax...  1.7 us
    pallas_call x1, Pallas kernels, body(): pl.pallas_call(lambda *refs: after_kernel(*refs, own=own), name='gradient...  1.65 us
  transfers between devices with their start and end apart: 2, of which 1 were waited for; matrix products, arithmetic and copies ran while one was open for 0% of the time, Pallas kernels for 1%

profile of v6, /device:TPU:1, one launch (start us, length us, event | category | flops | bytes accessed | tf_op | source)
XLA Modules:
  0.0 63.3 jit_solution(6997231436864202617)
XLA Ops:
  0.6 0.0 copy-start
  0.6 1.7 %kv_copies_and_loads.1 = (bf16[48,4,256]{2,1,0:T(4,128)(2,1)}, bf16[256,4096]{1,0:T(8,128)(2,1)S(1)}, bf16[128,256]{1,0:T(8,128)(2,1)S(1)}, f32[128,256]{1,0:T(8,128)S(1)}, s32[8,128]{1,0:T(8,128)S(1)}) custom-call(s32[2]{0:T(128)} %enc_hbm.1, s32[2]{0:T(128)} %dec_hbm.1, bf16[2,2,256]{2,1,0:T(2,128)(2,1)} %kv_hbm.1, bf16[256,4096]{1,0:T(8,128)(2,1)} %w_hbm.1, ...), custom_call_target="tpu_custom_call" | custom-call | tf_op jit(solution)/shard_map/kv_copies_and_loads/pallas_call | solution.py:172
  2.3 19.5 %all-to-all-start = ((bf16[48,4,256]{2,1,0:T(4,128)(2,1)}), bf16[48,4,256]{2,1,0:T(4,128)(2,1)S(1)}, u32[]{:S(2)}, u32[]{:S(2)}) async-start(bf16[48,4,256]{2,1,0:T(4,128)(2,1)} %get-tuple-element.15), calls=%async_computation | async-start | bytes 196608 | tf_op jit(solution)/shard_map/all_to_all | solution.py:91
  21.8 0.0 copy-done
  21.8 15.6 %all-gather = bf16[512,512]{1,0:T(8,128)(2,1)S(1)} all-gather(bf16[128,512]{1,0:T(8,128)(2,1)S(1)} %copy-done), channel_id=2, replica_groups={{0,2,4,6},{1,3,5,7},{8,10,12,14},{9,11,13,15},{16,18,20,22},{17,19,21,2..., dimensions={0}, use_global_device_ids=true | all-gather | bytes 655360 | tf_op jit(solution)/shard_map/all_gather | solution.py:97
  37.4 0.0 all-to-all-done
  37.5 7.0 %collective-permute-start = (bf16[4,128,512]{2,1,0:T(8,128)(2,1)S(1)}, bf16[4,128,512]{2,1,0:T(8,128)(2,1)S(1)}, u32[]{:S(2)}, u32[]{:S(2)}) collective-permute-start(bf16[4,128,512]{2,1,0:T(8,128)(2,1)S(1)} %bitcast.1), channel_id=1, source_target_pairs={{0,1},{1,0},{2,3},{3,2},{4,5},{5,4},{6,7},{7,6},{8,9},{9,8},{10,11... | collective-permute-start | bytes 1572872 | tf_op jit(solution)/shard_map/ppermute | solution.py:196
  44.5 0.8 %softmax_and_own_columns.1 = (f32[128,256]{1,0:T(8,128)S(1)}, f32[128,192]{1,0:T(8,128)S(1)}, bf16[128,192]{1,0:T(8,128)(2,1)S(1)}, bf16[192,256]{1,0:T(8,128)(2,1)S(1)}) custom-call(s32[8,128]{1,0:T(8,128)S(1)} %get-tuple-element.21.refs_0_, bf16[256,4096]{1,0:T(8,128)(2,1)S(1)} %get-tuple-element.18.refs_1_.refs_2_, ...), custom_call_target="tpu_custom_call" | custom-call | tf_op jit(solution)/shard_map/softmax_and_own_columns/pallas_call | solution.py:197
  45.3 0.7 %collective-permute-done.refs_0_ = bf16[4,128,512]{2,1,0:T(8,128)(2,1)S(1)} collective-permute-done((bf16[4,128,512]{2,1,0:T(8,128)(2,1)S(1)}, bf16[4,128,512]{2,1,0:T(8,128)(2,1)S(1)}, u32[]{:S(2)}, u32[]{:S(2)}) %collective-permute-start) | collective-permute-done | bytes 524320 | tf_op jit(solution)/shard_map/ppermute | solution.py:196
  46.0 1.6 %gradients.1 = (bf16[128,256]{1,0:T(8,128)(2,1)}, bf16[192,256]{1,0:T(8,128)(2,1)S(1)}) custom-call(bf16[4,128,512]{2,1,0:T(8,128)(2,1)S(1)} %collective-permute-done.refs_0_, bf16[192,256]{1,0:T(8,128)(2,1)S(1)} %reshape.10.refs_4_.refs_1_, bf16[256,4096]{1,0:T(8,128)(2,1)S(1)} %get-tuple-element.18.refs_1_.refs_2_, ...), custom_call_target="tpu_custom_call" | custom-call | tf_op jit(solution)/shard_map/gradients/pallas_call | solution.py:210
  47.7 15.0 %all_to_all.10.parts_ref = bf16[48,4,256]{2,1,0:T(4,128)(2,1)S(1)} all-to-all(bf16[48,4,256]{2,1,0:T(4,128)(2,1)S(1)} %reshape.11), channel_id=1, replica_groups={{240,232,224,216,208,200,192,184,176,168,160,152,144,136,128,120,112,10..., dimensions={0} | all-to-all | bytes 196608 | tf_op jit(solution)/shard_map/all_to_all | solution.py:91
  62.7 0.6 %sum_of_parts.1 = bf16[2,2,256]{2,1,0:T(2,128)(2,1)} custom-call(bf16[48,4,256]{2,1,0:T(4,128)(2,1)S(1)} %all_to_all.10.parts_ref), custom_call_target="tpu_custom_call" | custom-call | tf_op jit(solution)/shard_map/sum_of_parts/pallas_call | solution.py:130
  (2 shorter events, 0.1 us)
Async XLA Ops:
  0.6 21.2 %copy-start = (bf16[128,512]{1,0:T(8,128)(2,1)S(1)}, bf16[128,512]{1,0:T(8,128)(2,1)}, u32[]{:S(2)}) copy-start(bf16[128,512]{1,0:T(8,128)(2,1)} %param.8) | copy-start | bytes 393220
  2.3 35.1 %all-to-all-start = ((bf16[48,4,256]{2,1,0:T(4,128)(2,1)}), bf16[48,4,256]{2,1,0:T(4,128)(2,1)S(1)}, u32[]{:S(2)}, u32[]{:S(2)}) async-start(bf16[48,4,256]{2,1,0:T(4,128)(2,1)} %get-tuple-element.15), calls=%async_computation | async-start | bytes 196608 | tf_op jit(solution)/shard_map/all_to_all | solution.py:91
  37.5 8.5 %collective-permute-start = (bf16[4,128,512]{2,1,0:T(8,128)(2,1)S(1)}, bf16[4,128,512]{2,1,0:T(8,128)(2,1)S(1)}, u32[]{:S(2)}, u32[]{:S(2)}) collective-permute-start(bf16[4,128,512]{2,1,0:T(8,128)(2,1)S(1)} %bitcast.1), channel_id=1, source_target_pairs={{0,1},{1,0},{2,3},{3,2},{4,5},{5,4},{6,7},{7,6},{8,9},{9,8},{10,11... | collective-permute-start | bytes 1572872 | tf_op jit(solution)/shard_map/ppermute | solution.py:196

commit v7 on v5

--- a/solution.py
+++ b/solution.py
@@ -11,7 +11,7 @@
 VMEM = pl.BlockSpec(memory_space=pltpu.VMEM)
 HBM = pl.BlockSpec(memory_space=pltpu.HBM)
 PARAMS = pltpu.CompilerParams(vmem_limit_bytes=32 * 1024 * 1024)
-KV_FIRST = 24
+KV_FIRST = 35
 SUM_FIRST = 30
 CHIP_FIRST = 0
 

time: 64.1 us -> 63.7 us (level)
  no operation moved by 1% of the time
where the time goes in v7:
time: 63.7 us; the launch traced here: 62.9 us
  blocking collectives  30.4 us (48%)
  starting transfers between devices  26.3 us (41%)
  Pallas kernels  4.81 us (8%)
  waiting for transfers between devices  0.69 us (1%)
  between operations  0.68 us (1%)
    all_to_all x1, starting transfers between devices, exchange(): return lax.all_to_all(x, 'seq', 0, 0, tiled=True, axis_index_groups=[order])  19.8 us
    all_gather x1, blocking collectives, gather_chips(): return lax.all_gather(x, 'my', axis=0, axis_index_groups=[order])  15.6 us
    all_to_all x1, blocking collectives, exchange(): return lax.all_to_all(x, 'seq', 0, 0, tiled=True, axis_index_groups=[order])  14.8 us
    ppermute x1, starting transfers between devices, body(): og_other = lax.ppermute(og, 'mc', [(0, 1), (1, 0)])  6.43 us
    pallas_call x1, Pallas kernels, body(): pl.pallas_call(opening_kernel, name='kv_copies_and_loads', out_shape=(jax...  1.7 us
    pallas_call x1, Pallas kernels, body(): pl.pallas_call(lambda *refs: after_kernel(*refs, own=own), name='gradient...  1.65 us
  transfers between devices with their start and end apart: 2, of which 1 were waited for; matrix products, arithmetic and copies ran while one was open for 0% of the time, Pallas kernels for 1%

profile of v7, /device:TPU:1, one launch (start us, length us, event | category | flops | bytes accessed | tf_op | source)
XLA Modules:
  0.0 62.9 jit_solution(5431923059658090721)
XLA Ops:
  0.6 0.0 copy-start
  0.6 1.7 %kv_copies_and_loads.1 = (bf16[48,4,256]{2,1,0:T(4,128)(2,1)}, bf16[256,4096]{1,0:T(8,128)(2,1)S(1)}, bf16[128,256]{1,0:T(8,128)(2,1)S(1)}, f32[128,256]{1,0:T(8,128)S(1)}, s32[8,128]{1,0:T(8,128)S(1)}) custom-call(s32[2]{0:T(128)} %enc_hbm.1, s32[2]{0:T(128)} %dec_hbm.1, bf16[2,2,256]{2,1,0:T(2,128)(2,1)} %kv_hbm.1, bf16[256,4096]{1,0:T(8,128)(2,1)} %w_hbm.1, ...), custom_call_target="tpu_custom_call" | custom-call | tf_op jit(solution)/shard_map/kv_copies_and_loads/pallas_call | solution.py:172
  2.3 19.8 %all-to-all-start = ((bf16[48,4,256]{2,1,0:T(4,128)(2,1)}), bf16[48,4,256]{2,1,0:T(4,128)(2,1)S(1)}, u32[]{:S(2)}, u32[]{:S(2)}) async-start(bf16[48,4,256]{2,1,0:T(4,128)(2,1)} %get-tuple-element.15), calls=%async_computation | async-start | bytes 196608 | tf_op jit(solution)/shard_map/all_to_all | solution.py:91
  22.2 0.0 copy-done
  22.2 15.6 %all-gather = bf16[512,512]{1,0:T(8,128)(2,1)S(1)} all-gather(bf16[128,512]{1,0:T(8,128)(2,1)S(1)} %copy-done), channel_id=2, replica_groups={{0,2,4,6},{1,3,5,7},{8,10,12,14},{9,11,13,15},{16,18,20,22},{17,19,21,2..., dimensions={0}, use_global_device_ids=true | all-gather | bytes 655360 | tf_op jit(solution)/shard_map/all_gather | solution.py:97
  37.8 0.0 all-to-all-done
  37.9 6.4 %collective-permute-start = (bf16[4,128,512]{2,1,0:T(8,128)(2,1)S(1)}, bf16[4,128,512]{2,1,0:T(8,128)(2,1)S(1)}, u32[]{:S(2)}, u32[]{:S(2)}) collective-permute-start(bf16[4,128,512]{2,1,0:T(8,128)(2,1)S(1)} %bitcast.1), channel_id=1, source_target_pairs={{0,1},{1,0},{2,3},{3,2},{4,5},{5,4},{6,7},{7,6},{8,9},{9,8},{10,11... | collective-permute-start | bytes 1572872 | tf_op jit(solution)/shard_map/ppermute | solution.py:196
  44.3 0.8 %softmax_and_own_columns.1 = (f32[128,256]{1,0:T(8,128)S(1)}, f32[128,192]{1,0:T(8,128)S(1)}, bf16[128,192]{1,0:T(8,128)(2,1)S(1)}, bf16[192,256]{1,0:T(8,128)(2,1)S(1)}) custom-call(s32[8,128]{1,0:T(8,128)S(1)} %get-tuple-element.21.refs_0_, bf16[256,4096]{1,0:T(8,128)(2,1)S(1)} %get-tuple-element.18.refs_1_.refs_2_, ...), custom_call_target="tpu_custom_call" | custom-call | tf_op jit(solution)/shard_map/softmax_and_own_columns/pallas_call | solution.py:197
  45.1 0.7 %collective-permute-done.refs_0_ = bf16[4,128,512]{2,1,0:T(8,128)(2,1)S(1)} collective-permute-done((bf16[4,128,512]{2,1,0:T(8,128)(2,1)S(1)}, bf16[4,128,512]{2,1,0:T(8,128)(2,1)S(1)}, u32[]{:S(2)}, u32[]{:S(2)}) %collective-permute-start) | collective-permute-done | bytes 524320 | tf_op jit(solution)/shard_map/ppermute | solution.py:196
  45.8 1.6 %gradients.1 = (bf16[128,256]{1,0:T(8,128)(2,1)}, bf16[192,256]{1,0:T(8,128)(2,1)S(1)}) custom-call(bf16[4,128,512]{2,1,0:T(8,128)(2,1)S(1)} %collective-permute-done.refs_0_, bf16[192,256]{1,0:T(8,128)(2,1)S(1)} %reshape.10.refs_4_.refs_1_, bf16[256,4096]{1,0:T(8,128)(2,1)S(1)} %get-tuple-element.18.refs_1_.refs_2_, ...), custom_call_target="tpu_custom_call" | custom-call | tf_op jit(solution)/shard_map/gradients/pallas_call | solution.py:210
  47.5 14.8 %all_to_all.10.parts_ref = bf16[48,4,256]{2,1,0:T(4,128)(2,1)S(1)} all-to-all(bf16[48,4,256]{2,1,0:T(4,128)(2,1)S(1)} %reshape.11), channel_id=1, replica_groups={{240,248,256,264,272,280,288,296,304,312,320,328,336,344,352,360,368,37..., dimensions={0} | all-to-all | bytes 196608 | tf_op jit(solution)/shard_map/all_to_all | solution.py:91
  62.3 0.6 %sum_of_parts.1 = bf16[2,2,256]{2,1,0:T(2,128)(2,1)} custom-call(bf16[48,4,256]{2,1,0:T(4,128)(2,1)S(1)} %all_to_all.10.parts_ref), custom_call_target="tpu_custom_call" | custom-call | tf_op jit(solution)/shard_map/sum_of_parts/pallas_call | solution.py:130
  (2 shorter events, 0.1 us)
Async XLA Ops:
  0.6 21.6 %copy-start = (bf16[128,512]{1,0:T(8,128)(2,1)S(1)}, bf16[128,512]{1,0:T(8,128)(2,1)}, u32[]{:S(2)}) copy-start(bf16[128,512]{1,0:T(8,128)(2,1)} %param.8) | copy-start | bytes 393220
  2.3 35.5 %all-to-all-start = ((bf16[48,4,256]{2,1,0:T(4,128)(2,1)}), bf16[48,4,256]{2,1,0:T(4,128)(2,1)S(1)}, u32[]{:S(2)}, u32[]{:S(2)}) async-start(bf16[48,4,256]{2,1,0:T(4,128)(2,1)} %get-tuple-element.15), calls=%async_computation | async-start | bytes 196608 | tf_op jit(solution)/shard_map/all_to_all | solution.py:91
  37.9 8.0 %collective-permute-start = (bf16[4,128,512]{2,1,0:T(8,128)(2,1)S(1)}, bf16[4,128,512]{2,1,0:T(8,128)(2,1)S(1)}, u32[]{:S(2)}, u32[]{:S(2)}) collective-permute-start(bf16[4,128,512]{2,1,0:T(8,128)(2,1)S(1)} %bitcast.1), channel_id=1, source_target_pairs={{0,1},{1,0},{2,3},{3,2},{4,5},{5,4},{6,7},{7,6},{8,9},{9,8},{10,11... | collective-permute-start | bytes 1572872 | tf_op jit(solution)/shard_map/ppermute | solution.py:196
